TPU v7x, 32 devices: a whole 2x2x4 slice. The times are simulated.
32 devices in a mesh: grp: 16 (over z, x, core), mem: 2 (over y).
Axes of the slice: x: 2, y: 2, z: 4, core: 2. Of those that a mesh axis runs over, the one named last changes fastest.
Arguments:
- forcing: float32 [16, 256, 32, 128], P(None, 'grp', 'mem'), may hold values from -8 to 8
- aggregate: int32 [64, 8, 32], P('grp', 'mem'), may hold values from 0 to 8191, as said below
- factors: float32 [64, 128, 128], P('mem'), may hold values from -1.5 to 1.5, as said below
Outputs:
- solution: float32 [16, 256, 32, 128], P(None, 'grp', 'mem')
Inputs may be any that keep to these rules, and one draw needn't show every extreme that they name: Coarse unknowns are numbered over the fine blocks with the first block index taken modulo half the number of blocks along the first dimension, consecutive numbers lying close together in the other dimensions, so that an aggregate joins blocks of both halves of the grid; a few blocks take the entry of a block beside them. `factors`: each of the 64 blocks is lower triangular with its diagonal between 0.5 and 1.5.
All inputs are finite; a program needn't handle non-finite values.
Results may differ from a plain program's by a relative error of at most 0.00013.
Values sent between devices are 32-bit elements; how exact they have to be, the bound alone decides.
A program may use at most 128 MiB of HBM per device.

v0:
```python
import jax
import jax.numpy as jnp
from jax import lax
from jax.sharding import PartitionSpec as P

NC = 8192
PRE = 3
POST = 2


relaxation = 0.8


def with_halo(cells, sides, width):
    for axis, dim in sides:
        count = lax.axis_size(axis)
        ends = count - 1
        head = lax.slice_in_dim(cells, 0, width, axis=dim)
        tail = lax.slice_in_dim(cells, cells.shape[dim] - width, cells.shape[dim], axis=dim)
        cells = jnp.concatenate(
            [
                lax.ppermute(tail, axis, [(i, (i + 1) % count) for i in range(ends)]),
                cells,
                lax.ppermute(head, axis, [((i + 1) % count, i) for i in range(ends)]),
            ],
            axis=dim,
        )
    return cells


def stencil_inner(padded):
    centre = padded[:, 1:-1, 1:-1]
    beside = padded[:, 2:, 1:-1] + padded[:, :-2, 1:-1]
    beside = beside + padded[:, 1:-1, 2:] + padded[:, 1:-1, :-2]
    zeros_face = jnp.zeros(centre.shape[:3] + (1,), centre.dtype)
    upper_z = jnp.concatenate([centre[..., 1:], zeros_face], axis=3)
    lower_z = jnp.concatenate([zeros_face, centre[..., :-1]], axis=3)
    return 6.0 * centre - (beside + upper_z + lower_z)


def apply_operator(values):
    padded = with_halo(values, (("grp", 1), ("mem", 2)), 1)
    return stencil_inner(padded)


def restrict_blocks(residual, aggregate):
    blk_x, blk_y, blk_z = aggregate.shape
    sides = residual.shape[0]
    means = (
        residual.reshape(sides, blk_x, 4, blk_y, 4, blk_z, 4)
        .mean(axis=(2, 4, 6))
        .reshape(sides, -1)
    )
    summed = jax.ops.segment_sum(means.T, aggregate.reshape(-1), num_segments=NC)
    return summed.T


def prolong_blocks(coarse_fix, ids, valid):
    blk_x, blk_y, blk_z = ids.shape
    sides = coarse_fix.shape[0]
    picked = jnp.take(coarse_fix, ids.reshape(-1), axis=1) * valid.reshape(1, -1)
    picked = picked.reshape(sides, blk_x, 1, blk_y, 1, blk_z, 1)
    spread = jnp.broadcast_to(picked, (sides, blk_x, 4, blk_y, 4, blk_z, 4))
    return spread.reshape(sides, blk_x * 4, blk_y * 4, blk_z * 4)


def solve_blocks(coarse_rhs, factors):
    block_count = factors.shape[0]
    block_size = factors.shape[1]
    sides = coarse_rhs.shape[0]
    blocks = coarse_rhs.reshape(sides, block_count, block_size)
    inner = jnp.einsum("kbj,bij->kbi", blocks, factors, precision=lax.Precision.HIGHEST)
    result = jnp.einsum("kbi,bij->kbj", inner, factors, precision=lax.Precision.HIGHEST)
    return result.reshape(sides, block_count * block_size)


def shards(forcing, aggregate, factors):
    weight = relaxation / 6.0
    smoothed = weight * forcing
    for repeat in range(PRE - 1):
        smoothed = smoothed + weight * (forcing - apply_operator(smoothed))
    residual = forcing - apply_operator(smoothed)
    partial_value = restrict_blocks(residual, aggregate)
    coarse_rhs = lax.psum(partial_value, ("grp", "mem"))
    all_factors = lax.all_gather(factors, "mem", axis=0, tiled=True)
    coarse_fix = solve_blocks(coarse_rhs, all_factors)
    lifted = prolong_blocks(coarse_fix, aggregate, jnp.ones(aggregate.shape, jnp.float32))
    correction = lifted - weight * apply_operator(lifted)
    solution = smoothed + correction
    for repeat in range(POST):
        solution = solution + weight * (forcing - apply_operator(solution))
    return solution


def solution(mesh):
    placed = (P(None, "grp", "mem", None), P("grp", "mem", None), P("mem", None, None))
    return jax.shard_map(
        shards, mesh=mesh, in_specs=placed, out_specs=P(None, "grp", "mem", None), check_vma=False
    )
```

profile of v0, /device:TPU:8, one launch (start us, length us, event | category | flops | bytes accessed | tf_op | source)
XLA Modules:
  0.0 380.2 jit_solution(7049673006676737177)
XLA Ops:
  9.2 2.7 collective-permute-start
  14.4 4.7 %collective-permute-done.1 = f32[16,1,16,128]{3,2,1,0:T(8,128)S(1)} collective-permute-done((f32[16,1,16,128]{3,2,1,0:T(8,128)S(1)}, f32[16,1,16,128]{3,2,1,0:T(8,128)S(1)}, u32[]{:S(2)}, u32[]{:S(2)}) %collective-permute-start.1) | collective-permute-done | bytes 131104 | tf_op jit(solution)/shard_map/ppermute | solution.py:22
  19.3 3.4 collective-permute-start.3
  25.6 4.4 %collective-permute-done.2 = f32[16,18,1,128]{3,0,2,1:T(8,128)S(1)} collective-permute-done((f32[16,18,1,128]{3,0,2,1:T(8,128)S(1)}, f32[16,18,1,128]{3,0,2,1:T(8,128)S(1)}, u32[]{:S(2)}, u32[]{:S(2)}) %collective-permute-start.2) | collective-permute-done | bytes 147488 | tf_op jit(solution)/shard_map/ppermute | solution.py:24
  34.2 2.4 collective-permute-start.5
  36.7 4.7 %collective-permute-done.5 = f32[16,1,16,128]{3,2,1,0:T(8,128)S(1)} collective-permute-done((f32[16,1,16,128]{3,2,1,0:T(8,128)S(1)}, f32[16,1,16,128]{3,2,1,0:T(8,128)S(1)}, u32[]{:S(2)}, u32[]{:S(2)}) %collective-permute-start.5) | collective-permute-done | bytes 131104 | tf_op jit(solution)/shard_map/ppermute | solution.py:22
  45.9 4.3 %collective-permute-done.6 = f32[16,18,1,128]{3,0,2,1:T(8,128)S(1)} collective-permute-done((f32[16,18,1,128]{3,0,2,1:T(8,128)S(1)}, f32[16,18,1,128]{3,0,2,1:T(8,128)S(1)}, u32[]{:S(2)}, u32[]{:S(2)}) %collective-permute-start.6) | collective-permute-done | bytes 147488 | tf_op jit(solution)/shard_map/ppermute | solution.py:24
  54.3 2.4 collective-permute-start.9
  56.8 4.7 %collective-permute-done.9 = f32[16,1,16,128]{3,2,1,0:T(8,128)S(1)} collective-permute-done((f32[16,1,16,128]{3,2,1,0:T(8,128)S(1)}, f32[16,1,16,128]{3,2,1,0:T(8,128)S(1)}, u32[]{:S(2)}, u32[]{:S(2)}) %collective-permute-start.9) | collective-permute-done | bytes 131104 | tf_op jit(solution)/shard_map/ppermute | solution.py:22
  66.0 4.4 %collective-permute-done.10 = f32[16,18,1,128]{3,0,2,1:T(8,128)S(1)} collective-permute-done((f32[16,18,1,128]{3,0,2,1:T(8,128)S(1)}, f32[16,18,1,128]{3,0,2,1:T(8,128)S(1)}, u32[]{:S(2)}, u32[]{:S(2)}) %collective-permute-start.10) | collective-permute-done | bytes 147488 | tf_op jit(solution)/shard_map/ppermute | solution.py:24
  70.5 2.8 fusion.31
  73.4 10.0 %copy.356 = f32[16,16,16,128]{0,3,2,1:T(8,128)} copy(f32[16,16,16,128]{3,2,1,0:T(8,128)} %fusion.31) | data formatting | bytes 4194304 | tf_op jit(solution)/shard_map/sub | solution.py:82
  83.4 9.4 %reduce_sum.9 = f32[16,4,4,32]{0,3,2,1:T(8,128)S(1)} reduce(f32[16,4,4,4,4,32,4]{0,6,5,4,3,2,1:T(4,128)} %bitcast.23, f32[]{:T(128)} %constant.11.clone.1), dimensions={2,4,6}, to_apply=%region_0.0 | reduce | flops 516096 | bytes 2129924 | tf_op jit(solution)/shard_map/reduce_sum | solution.py:51
  92.8 4.4 %scatter_custom_fusion = f32[8192,16]{1,0:T(8,128)} fusion(s32[512]{0:T(512)S(1)} %reshape.77, f32[512,16]{1,0:T(8,128)S(1)} %bitcast.27, f32[]{:T(128)} %constant.11.clone.1), kind=kCustom, calls=%fused_computation.102 | custom fusion | flops 8192 | bytes 524292 | tf_op jit(solution)/shard_map/scatter-add | solution.py:54
  97.2 3.5 copy.358
  101.4 166.7 %all-reduce.14.cloned.1.call-done = f32[16,64,128]{2,0,1:T(8,128)} async-done(((f32[16,64,128]{2,0,1:T(8,128)}), f32[16,64,128]{2,0,1:T(8,128)}) %all-reduce.14.cloned.1.call-update) | async-done | bytes 524304 | tf_op jit(solution)/shard_map/psum | solution.py:84
  268.1 8.6 %convolution_bitcast_fusion.1 = f32[16,64,128]{2,0,1:T(8,128)S(1)} fusion(f32[16,64,128]{2,0,1:T(8,128)} %all-reduce.14.cloned.1.call-done, f32[64,128,128]{2,1,0:T(8,128)} %all-gather.2.cloned.1.call-done), kind=kOutput, calls=%fused_computation.105 | convolution fusion | flops 201326592 | bytes 5242880 | tf_op jit(solution)/shard_map/kbj,bij->kbi/dot_general | solution.py:72
  276.8 3.8 convolution_bitcast_fusion
  280.6 2.6 copy.384
  283.2 3.2 gather_fusion
  286.5 3.9 %broadcast_in_dim.21 = f32[16,4,4,4,4,32,4]{0,6,5,4,3,2,1:T(4,128)S(1)} broadcast(f32[16,4,4,32]{0,3,2,1:T(8,128)S(1)} %broadcast_select_fusion), dimensions={0,1,3,5} | broadcast | bytes 2129920 | tf_op jit(solution)/shard_map/broadcast_in_dim | solution.py:63
  290.4 5.7 %copy-done = f32[16,4,4,4,4,32,4]{0,6,5,4,3,2,1:T(4,128)} copy-done((f32[16,4,4,4,4,32,4]{0,6,5,4,3,2,1:T(4,128)}, f32[16,4,4,4,4,32,4]{0,6,5,4,3,2,1:T(4,128)S(1)}, u32[]{:S(2)}) %copy-start) | copy-done | bytes 2097176
  303.5 11.0 %copy.373 = f32[16,16,16,128]{3,2,1,0:T(8,128)} copy(f32[16,16,16,128]{0,3,2,1:T(8,128)} %bitcast.22) | data formatting | bytes 4194304 | tf_op jit(solution)/shard_map/reshape | solution.py:64
  316.5 3.4 collective-permute-start.15
  323.5 4.0 %collective-permute-done.14 = f32[16,18,1,128]{3,0,2,1:T(8,128)S(1)} collective-permute-done((f32[16,18,1,128]{3,0,2,1:T(8,128)S(1)}, f32[16,18,1,128]{3,0,2,1:T(8,128)S(1)}, u32[]{:S(2)}, u32[]{:S(2)}) %collective-permute-start.14) | collective-permute-done | bytes 147488 | tf_op jit(solution)/shard_map/ppermute | solution.py:24
  329.6 3.8 %collective-permute-start.16 = (f32[16,1,16,128]{3,2,1,0:T(8,128)S(1)}, f32[16,1,16,128]{3,2,1,0:T(8,128)S(1)}, u32[]{:S(2)}, u32[]{:S(2)}) collective-permute-start(f32[16,1,16,128]{3,2,1,0:T(8,128)S(1)} %get-tuple-element.26), channel_id=1, source_target_pairs={{2,0},{4,2},{6,4},{8,6},{10,8},{12,10},{14,12},{16,14},{18,16},{20... | collective-permute-start | bytes 393224 | tf_op jit(solution)/shard_map/ppermute | solution.py:24
  336.0 4.7 %collective-permute-done.17 = f32[16,1,16,128]{3,2,1,0:T(8,128)S(1)} collective-permute-done((f32[16,1,16,128]{3,2,1,0:T(8,128)S(1)}, f32[16,1,16,128]{3,2,1,0:T(8,128)S(1)}, u32[]{:S(2)}, u32[]{:S(2)}) %collective-permute-start.17) | collective-permute-done | bytes 131104 | tf_op jit(solution)/shard_map/ppermute | solution.py:22
  345.1 4.4 %collective-permute-done.18 = f32[16,18,1,128]{3,0,2,1:T(8,128)S(1)} collective-permute-done((f32[16,18,1,128]{3,0,2,1:T(8,128)S(1)}, f32[16,18,1,128]{3,0,2,1:T(8,128)S(1)}, u32[]{:S(2)}, u32[]{:S(2)}) %collective-permute-start.18) | collective-permute-done | bytes 147488 | tf_op jit(solution)/shard_map/ppermute | solution.py:24
  353.7 2.4 collective-permute-start.21
  356.2 4.7 %collective-permute-done.21 = f32[16,1,16,128]{3,2,1,0:T(8,128)S(1)} collective-permute-done((f32[16,1,16,128]{3,2,1,0:T(8,128)S(1)}, f32[16,1,16,128]{3,2,1,0:T(8,128)S(1)}, u32[]{:S(2)}, u32[]{:S(2)}) %collective-permute-start.21) | collective-permute-done | bytes 131104 | tf_op jit(solution)/shard_map/ppermute | solution.py:22
  365.4 4.3 %collective-permute-done.22 = f32[16,18,1,128]{3,0,2,1:T(8,128)S(1)} collective-permute-done((f32[16,18,1,128]{3,0,2,1:T(8,128)S(1)}, f32[16,18,1,128]{3,0,2,1:T(8,128)S(1)}, u32[]{:S(2)}, u32[]{:S(2)}) %collective-permute-start.22) | collective-permute-done | bytes 147488 | tf_op jit(solution)/shard_map/ppermute | solution.py:24
  369.8 3.0 fusion.6
  (104 shorter events, 56.4 us)
Async XLA Ops:
  7.4 260.8 %all-reduce.14.cloned.1.call-start = ((), (), s32[]{:S(2)}) async-start(), calls=%async_computation | async-start | bytes 1048576 | tf_op jit(solution)/shard_map/psum | solution.py:84
  9.2 5.2 %collective-permute-start = (f32[16,1,16,128]{3,2,1,0:T(8,128)S(1)}, f32[16,1,16,128]{3,2,1,0:T(8,128)S(1)}, u32[]{:S(2)}, u32[]{:S(2)}) collective-permute-start(f32[16,1,16,128]{3,2,1,0:T(8,128)S(1)} %get-tuple-element.40), channel_id=1, source_target_pairs={{2,0},{4,2},{6,4},{8,6},{10,8},{12,10},{14,12},{16,14},{18,16},{20... | collective-permute-start | bytes 393224 | tf_op jit(solution)/shard_map/ppermute | solution.py:24
  11.9 7.2 %collective-permute-start.1 = (f32[16,1,16,128]{3,2,1,0:T(8,128)S(1)}, f32[16,1,16,128]{3,2,1,0:T(8,128)S(1)}, u32[]{:S(2)}, u32[]{:S(2)}) collective-permute-start(f32[16,1,16,128]{3,2,1,0:T(8,128)S(1)} %get-tuple-element.39), channel_id=1, source_target_pairs={{0,2},{2,4},{4,6},{6,8},{8,10},{10,12},{12,14},{14,16},{16,18},{18... | collective-permute-start | bytes 393224 | tf_op jit(solution)/shard_map/ppermute | solution.py:22
  19.3 6.1 %collective-permute-start.3 = (f32[16,18,1,128]{3,0,2,1:T(8,128)S(1)}, f32[16,18,1,128]{3,0,2,1:T(8,128)S(1)}, u32[]{:S(2)}, u32[]{:S(2)}) collective-permute-start(f32[16,18,1,128]{3,0,2,1:T(8,128)S(1)} %copy.346), channel_id=1, source_target_pairs={{0,1},{2,3},{4,5},{6,7},{8,9},{10,11},{12,13},{14,15},{16,17},{18,... | collective-permute-start | bytes 442376 | tf_op jit(solution)/shard_map/ppermute | solution.py:22
  22.8 7.3 %copy-start.1 = (f32[16,16,16,128]{3,2,1,0:T(8,128)S(1)}, f32[16,16,16,128]{3,2,1,0:T(8,128)}, u32[]{:S(2)}) copy-start(f32[16,16,16,128]{3,2,1,0:T(8,128)} %param.3) | copy-start | bytes 6291460
  22.8 7.2 %collective-permute-start.2 = (f32[16,18,1,128]{3,0,2,1:T(8,128)S(1)}, f32[16,18,1,128]{3,0,2,1:T(8,128)S(1)}, u32[]{:S(2)}, u32[]{:S(2)}) collective-permute-start(f32[16,18,1,128]{3,0,2,1:T(8,128)S(1)} %copy.344), channel_id=1, source_target_pairs={{1,0},{3,2},{5,4},{7,6},{9,8},{11,10},{13,12},{15,14},{17,16},{19,... | collective-permute-start | bytes 442376 | tf_op jit(solution)/shard_map/ppermute | solution.py:24
  32.2 4.4 %collective-permute-start.4 = (f32[16,1,16,128]{3,2,1,0:T(8,128)S(1)}, f32[16,1,16,128]{3,2,1,0:T(8,128)S(1)}, u32[]{:S(2)}, u32[]{:S(2)}) collective-permute-start(f32[16,1,16,128]{3,2,1,0:T(8,128)S(1)} %get-tuple-element.36), channel_id=1, source_target_pairs={{2,0},{4,2},{6,4},{8,6},{10,8},{12,10},{14,12},{16,14},{18,16},{20... | collective-permute-start | bytes 393224 | tf_op jit(solution)/shard_map/ppermute | solution.py:24
  34.2 7.2 %collective-permute-start.5 = (f32[16,1,16,128]{3,2,1,0:T(8,128)S(1)}, f32[16,1,16,128]{3,2,1,0:T(8,128)S(1)}, u32[]{:S(2)}, u32[]{:S(2)}) collective-permute-start(f32[16,1,16,128]{3,2,1,0:T(8,128)S(1)} %get-tuple-element.35), channel_id=1, source_target_pairs={{0,2},{2,4},{4,6},{6,8},{8,10},{10,12},{12,14},{14,16},{16,18},{18... | collective-permute-start | bytes 393224 | tf_op jit(solution)/shard_map/ppermute | solution.py:22
  41.6 4.1 %collective-permute-start.7 = (f32[16,18,1,128]{3,0,2,1:T(8,128)S(1)}, f32[16,18,1,128]{3,0,2,1:T(8,128)S(1)}, u32[]{:S(2)}, u32[]{:S(2)}) collective-permute-start(f32[16,18,1,128]{3,0,2,1:T(8,128)S(1)} %copy.350), channel_id=1, source_target_pairs={{0,1},{2,3},{4,5},{6,7},{8,9},{10,11},{12,13},{14,15},{16,17},{18,... | collective-permute-start | bytes 442376 | tf_op jit(solution)/shard_map/ppermute | solution.py:22
  43.1 7.0 %collective-permute-start.6 = (f32[16,18,1,128]{3,0,2,1:T(8,128)S(1)}, f32[16,18,1,128]{3,0,2,1:T(8,128)S(1)}, u32[]{:S(2)}, u32[]{:S(2)}) collective-permute-start(f32[16,18,1,128]{3,0,2,1:T(8,128)S(1)} %copy.348), channel_id=1, source_target_pairs={{1,0},{3,2},{5,4},{7,6},{9,8},{11,10},{13,12},{15,14},{17,16},{19,... | collective-permute-start | bytes 442376 | tf_op jit(solution)/shard_map/ppermute | solution.py:24
  50.3 6.4 %copy-start.6 = (s32[4,4,32]{2,1,0:T(4,128)S(1)}, s32[4,4,32]{2,1,0:T(4,128)}, u32[]{:S(2)}) copy-start(s32[4,4,32]{2,1,0:T(4,128)} %param.4) | copy-start | bytes 6148
  52.3 4.4 %collective-permute-start.8 = (f32[16,1,16,128]{3,2,1,0:T(8,128)S(1)}, f32[16,1,16,128]{3,2,1,0:T(8,128)S(1)}, u32[]{:S(2)}, u32[]{:S(2)}) collective-permute-start(f32[16,1,16,128]{3,2,1,0:T(8,128)S(1)} %get-tuple-element.32), channel_id=1, source_target_pairs={{2,0},{4,2},{6,4},{8,6},{10,8},{12,10},{14,12},{16,14},{18,16},{20... | collective-permute-start | bytes 393224 | tf_op jit(solution)/shard_map/ppermute | solution.py:24
  54.3 7.2 %collective-permute-start.9 = (f32[16,1,16,128]{3,2,1,0:T(8,128)S(1)}, f32[16,1,16,128]{3,2,1,0:T(8,128)S(1)}, u32[]{:S(2)}, u32[]{:S(2)}) collective-permute-start(f32[16,1,16,128]{3,2,1,0:T(8,128)S(1)} %get-tuple-element.31), channel_id=1, source_target_pairs={{0,2},{2,4},{4,6},{6,8},{8,10},{10,12},{12,14},{14,16},{16,18},{18... | collective-permute-start | bytes 393224 | tf_op jit(solution)/shard_map/ppermute | solution.py:22
  61.7 4.1 %collective-permute-start.11 = (f32[16,18,1,128]{3,0,2,1:T(8,128)S(1)}, f32[16,18,1,128]{3,0,2,1:T(8,128)S(1)}, u32[]{:S(2)}, u32[]{:S(2)}) collective-permute-start(f32[16,18,1,128]{3,0,2,1:T(8,128)S(1)} %copy.354), channel_id=1, source_target_pairs={{0,1},{2,3},{4,5},{6,7},{8,9},{10,11},{12,13},{14,15},{16,17},{18,... | collective-permute-start | bytes 442376 | tf_op jit(solution)/shard_map/ppermute | solution.py:22
  63.2 7.3 %copy-start.2 = (f32[16,16,16,128]{3,2,1,0:T(8,128)S(1)}, f32[16,16,16,128]{3,2,1,0:T(8,128)}, u32[]{:S(2)}) copy-start(f32[16,16,16,128]{3,2,1,0:T(8,128)} %param.3) | copy-start | bytes 6291460
  63.2 7.2 %collective-permute-start.10 = (f32[16,18,1,128]{3,0,2,1:T(8,128)S(1)}, f32[16,18,1,128]{3,0,2,1:T(8,128)S(1)}, u32[]{:S(2)}, u32[]{:S(2)}) collective-permute-start(f32[16,18,1,128]{3,0,2,1:T(8,128)S(1)} %copy.352), channel_id=1, source_target_pairs={{1,0},{3,2},{5,4},{7,6},{9,8},{11,10},{13,12},{15,14},{17,16},{19,... | collective-permute-start | bytes 442376 | tf_op jit(solution)/shard_map/ppermute | solution.py:24
  100.7 167.4 %all-gather.2.cloned.1.call-start = ((), (), s32[]{:S(2)}) async-start(), calls=%async_computation.1 | async-start | bytes 6291456 | tf_op jit(solution)/shard_map/all_gather | solution.py:85
  268.1 8.6 %copy-start.5 = (f32[64,128,128]{2,1,0:T(8,128)S(1)}, f32[64,128,128]{2,1,0:T(8,128)}, u32[]{:S(2)}) copy-start(f32[64,128,128]{2,1,0:T(8,128)} %all-gather.2.cloned.1.call-done) | copy-start | bytes 12582916
  298.9 15.7 %collective-permute-start.12 = (f32[16,1,16,128]{3,2,1,0:T(8,128)S(1)}, f32[16,1,16,128]{3,2,1,0:T(8,128)S(1)}, u32[]{:S(2)}, u32[]{:S(2)}) collective-permute-start(f32[16,1,16,128]{3,2,1,0:T(8,128)S(1)} %copy.362), channel_id=1, source_target_pairs={{2,0},{4,2},{6,4},{8,6},{10,8},{12,10},{14,12},{16,14},{18,16},{20... | collective-permute-start | bytes 393224 | tf_op jit(solution)/shard_map/ppermute | solution.py:24
  301.2 13.3 %collective-permute-start.13 = (f32[16,1,16,128]{3,2,1,0:T(8,128)S(1)}, f32[16,1,16,128]{3,2,1,0:T(8,128)S(1)}, u32[]{:S(2)}, u32[]{:S(2)}) collective-permute-start(f32[16,1,16,128]{3,2,1,0:T(8,128)S(1)} %copy.364), channel_id=1, source_target_pairs={{0,2},{2,4},{4,6},{6,8},{8,10},{10,12},{12,14},{14,16},{16,18},{18... | collective-permute-start | bytes 393224 | tf_op jit(solution)/shard_map/ppermute | solution.py:22
  314.5 6.7 %copy-start.4 = (f32[16,16,16,128]{3,2,1,0:T(8,128)S(1)}, f32[16,16,16,128]{3,2,1,0:T(8,128)}, u32[]{:S(2)}) copy-start(f32[16,16,16,128]{3,2,1,0:T(8,128)} %copy.373) | copy-start | bytes 6291460
  316.5 6.8 %collective-permute-start.15 = (f32[16,18,1,128]{3,0,2,1:T(8,128)S(1)}, f32[16,18,1,128]{3,0,2,1:T(8,128)S(1)}, u32[]{:S(2)}, u32[]{:S(2)}) collective-permute-start(f32[16,18,1,128]{3,0,2,1:T(8,128)S(1)} %copy.369), channel_id=1, source_target_pairs={{0,1},{2,3},{4,5},{6,7},{8,9},{10,11},{12,13},{14,15},{16,17},{18,... | collective-permute-start | bytes 442376 | tf_op jit(solution)/shard_map/ppermute | solution.py:22
  319.9 7.5 %collective-permute-start.14 = (f32[16,18,1,128]{3,0,2,1:T(8,128)S(1)}, f32[16,18,1,128]{3,0,2,1:T(8,128)S(1)}, u32[]{:S(2)}, u32[]{:S(2)}) collective-permute-start(f32[16,18,1,128]{3,0,2,1:T(8,128)S(1)} %copy.367), channel_id=1, source_target_pairs={{1,0},{3,2},{5,4},{7,6},{9,8},{11,10},{13,12},{15,14},{17,16},{19,... | collective-permute-start | bytes 442376 | tf_op jit(solution)/shard_map/ppermute | solution.py:24
  329.6 6.3 %collective-permute-start.16 = (f32[16,1,16,128]{3,2,1,0:T(8,128)S(1)}, f32[16,1,16,128]{3,2,1,0:T(8,128)S(1)}, u32[]{:S(2)}, u32[]{:S(2)}) collective-permute-start(f32[16,1,16,128]{3,2,1,0:T(8,128)S(1)} %get-tuple-element.26), channel_id=1, source_target_pairs={{2,0},{4,2},{6,4},{8,6},{10,8},{12,10},{14,12},{16,14},{18,16},{20... | collective-permute-start | bytes 393224 | tf_op jit(solution)/shard_map/ppermute | solution.py:24
  333.5 7.2 %collective-permute-start.17 = (f32[16,1,16,128]{3,2,1,0:T(8,128)S(1)}, f32[16,1,16,128]{3,2,1,0:T(8,128)S(1)}, u32[]{:S(2)}, u32[]{:S(2)}) collective-permute-start(f32[16,1,16,128]{3,2,1,0:T(8,128)S(1)} %get-tuple-element.25), channel_id=1, source_target_pairs={{0,2},{2,4},{4,6},{6,8},{8,10},{10,12},{12,14},{14,16},{16,18},{18... | collective-permute-start | bytes 393224 | tf_op jit(solution)/shard_map/ppermute | solution.py:22
  340.9 4.1 %collective-permute-start.19 = (f32[16,18,1,128]{3,0,2,1:T(8,128)S(1)}, f32[16,18,1,128]{3,0,2,1:T(8,128)S(1)}, u32[]{:S(2)}, u32[]{:S(2)}) collective-permute-start(f32[16,18,1,128]{3,0,2,1:T(8,128)S(1)} %copy.376), channel_id=1, source_target_pairs={{0,1},{2,3},{4,5},{6,7},{8,9},{10,11},{12,13},{14,15},{16,17},{18,... | collective-permute-start | bytes 442376 | tf_op jit(solution)/shard_map/ppermute | solution.py:22
  342.4 7.3 %copy-start.3 = (f32[16,16,16,128]{3,2,1,0:T(8,128)S(1)}, f32[16,16,16,128]{3,2,1,0:T(8,128)}, u32[]{:S(2)}) copy-start(f32[16,16,16,128]{3,2,1,0:T(8,128)} %param.3) | copy-start | bytes 6291460
  342.4 7.2 %collective-permute-start.18 = (f32[16,18,1,128]{3,0,2,1:T(8,128)S(1)}, f32[16,18,1,128]{3,0,2,1:T(8,128)S(1)}, u32[]{:S(2)}, u32[]{:S(2)}) collective-permute-start(f32[16,18,1,128]{3,0,2,1:T(8,128)S(1)} %copy.374), channel_id=1, source_target_pairs={{1,0},{3,2},{5,4},{7,6},{9,8},{11,10},{13,12},{15,14},{17,16},{19,... | collective-permute-start | bytes 442376 | tf_op jit(solution)/shard_map/ppermute | solution.py:24
  351.8 4.4 %collective-permute-start.20 = (f32[16,1,16,128]{3,2,1,0:T(8,128)S(1)}, f32[16,1,16,128]{3,2,1,0:T(8,128)S(1)}, u32[]{:S(2)}, u32[]{:S(2)}) collective-permute-start(f32[16,1,16,128]{3,2,1,0:T(8,128)S(1)} %get-tuple-element.22), channel_id=1, source_target_pairs={{2,0},{4,2},{6,4},{8,6},{10,8},{12,10},{14,12},{16,14},{18,16},{20... | collective-permute-start | bytes 393224 | tf_op jit(solution)/shard_map/ppermute | solution.py:24
  353.7 7.2 %collective-permute-start.21 = (f32[16,1,16,128]{3,2,1,0:T(8,128)S(1)}, f32[16,1,16,128]{3,2,1,0:T(8,128)S(1)}, u32[]{:S(2)}, u32[]{:S(2)}) collective-permute-start(f32[16,1,16,128]{3,2,1,0:T(8,128)S(1)} %get-tuple-element.21), channel_id=1, source_target_pairs={{0,2},{2,4},{4,6},{6,8},{8,10},{10,12},{12,14},{14,16},{16,18},{18... | collective-permute-start | bytes 393224 | tf_op jit(solution)/shard_map/ppermute | solution.py:22
  361.1 4.1 %collective-permute-start.23 = (f32[16,18,1,128]{3,0,2,1:T(8,128)S(1)}, f32[16,18,1,128]{3,0,2,1:T(8,128)S(1)}, u32[]{:S(2)}, u32[]{:S(2)}) collective-permute-start(f32[16,18,1,128]{3,0,2,1:T(8,128)S(1)} %copy.380), channel_id=1, source_target_pairs={{0,1},{2,3},{4,5},{6,7},{8,9},{10,11},{12,13},{14,15},{16,17},{18,... | collective-permute-start | bytes 442376 | tf_op jit(solution)/shard_map/ppermute | solution.py:22
  362.6 7.0 %collective-permute-start.22 = (f32[16,18,1,128]{3,0,2,1:T(8,128)S(1)}, f32[16,18,1,128]{3,0,2,1:T(8,128)S(1)}, u32[]{:S(2)}, u32[]{:S(2)}) collective-permute-start(f32[16,18,1,128]{3,0,2,1:T(8,128)S(1)} %copy.378), channel_id=1, source_target_pairs={{1,0},{3,2},{5,4},{7,6},{9,8},{11,10},{13,12},{15,14},{17,16},{19,... | collective-permute-start | bytes 442376 | tf_op jit(solution)/shard_map/ppermute | solution.py:24
  (1 other events, 5.8 us)
Sparse Core Ops, SparseCore 0:
  100.8 167.2 all-reduce.13
Sparse Core Ops, SparseCore 1:
  102.7 56.0 all-gather.1
where the time goes:
time: 381 us; the launch traced here: 380 us
  waiting for transfers between devices  221 us (58%)
  local copies, waits for them, and re-layouts  49.7 us (13%)
  starting transfers between devices  48.9 us (13%)
  other arithmetic  32.7 us (9%)
  between operations  15.5 us (4%)
  matrix products  12.4 us (3%)
    psum x1, waiting for transfers between devices, shards(): coarse_rhs = lax.psum(partial_value, ('grp', 'mem'))  167 us
    ppermute x12, waiting for transfers between devices, with_halo(): lax.ppermute(tail, axis, [(i, (i + 1) % count) for i in range(ends)])  27 us
    ppermute x12, waiting for transfers between devices, with_halo(): lax.ppermute(head, axis, [((i + 1) % count, i) for i in range(ends)])  27 us
    ppermute x12, starting transfers between devices, with_halo(): lax.ppermute(tail, axis, [(i, (i + 1) % count) for i in range(ends)])  26.1 us
    ppermute x12, starting transfers between devices, with_halo(): lax.ppermute(head, axis, [((i + 1) % count, i) for i in range(ends)])  22.7 us
    reshape x1, local copies, waits for them, and re-layouts, prolong_blocks(): return spread.reshape(sides, blk_x * 4, blk_y * 4, blk_z * 4)  11 us
    sub x1, local copies, waits for them, and re-layouts, shards(): residual = forcing - apply_operator(smoothed)  10 us
    reduce_sum x1, other arithmetic, restrict_blocks(): means = residual.reshape(sides, blk_x, 4, blk_y, 4, blk_z, 4).mean(axis=(...  9.37 us
  transfers between devices with their start and end apart: 26, of which 22 were waited for; matrix products, arithmetic and copies ran while one was open for 4% of the time, Pallas kernels for 0%

commit v1 on v0

v1 whole, which is shorter than its diff:
```python
import functools

import jax
import jax.numpy as jnp
from jax import lax
from jax.experimental import pallas as pl
from jax.experimental.pallas import tpu as pltpu
from jax.sharding import PartitionSpec as P

NC = 8192
relaxation = 0.8
WEIGHT = relaxation / 6.0
CELL = 4
HALO = 4
F32 = jnp.float32
BF16 = jnp.bfloat16
MESH = pl.DeviceIdType.MESH
VMEM = pltpu.VMEM


def vmem_spec():
    return pl.BlockSpec(memory_space=pltpu.VMEM)


def params(**kw):
    return pltpu.CompilerParams(vmem_limit_bytes=60 * 1024 * 1024, **kw)


def pieces(value):
    hi = value.astype(BF16)
    rest = value - hi.astype(F32)
    mid = rest.astype(BF16)
    low = (rest - mid.astype(F32)).astype(BF16)
    return jnp.concatenate([hi, mid, low], axis=0)


def joined(value):
    k = value.shape[0] // 3
    return value[:k] + (value[k : 2 * k] + value[2 * k :])


def halo_kernel(G, M, f_ref, a_ref, fe, ae, sx, rx, sy, ry):
    K, X, Y, Z = f_ref.shape
    bx, by = X // CELL, Y // CELL
    g, m = lax.axis_index("grp"), lax.axis_index("mem")
    flat = f_ref.reshape(K * X * Y, Z)

    sides = []
    if G > 1:
        sides += [(g > 0, {"grp": g - 1}), (g < G - 1, {"grp": g + 1})]
    if M > 1:
        sides += [(m > 0, {"mem": m - 1}), (m < M - 1, {"mem": m + 1})]
    barrier = pltpu.get_barrier_semaphore()
    for there, dev in sides:

        @pl.when(there)
        def _(dev=dev):
            pl.semaphore_signal(barrier, inc=1, device_id=dev, device_id_type=MESH)

    @pl.loop(0, X)
    def _(x):
        for y in range(Y):
            fe[HALO + x, HALO + y] = flat[pl.ds(x * Y + y, K, stride=X * Y), :]

    ae[1 : 1 + bx, 1 : 1 + by] = a_ref[...]

    def blank(start):
        @pl.loop(start, start + HALO)
        def _(x):
            fe[x, HALO : HALO + Y] = jnp.zeros((Y,) + fe.shape[2:], F32)

    @pl.when(g == 0)
    def _():
        blank(0)
        ae[0:1, 1 : 1 + by] = jnp.zeros((1, by) + ae.shape[2:], jnp.int32)

    @pl.when(g == G - 1)
    def _():
        blank(HALO + X)
        ae[1 + bx :, 1 : 1 + by] = jnp.zeros((1, by) + ae.shape[2:], jnp.int32)

    @pl.when(m == 0)
    def _():
        @pl.loop(0, X + 2 * HALO)
        def _(x):
            fe[x, 0:HALO] = jnp.zeros((HALO,) + fe.shape[2:], F32)

        ae[:, 0:1] = jnp.zeros((bx + 2, 1) + ae.shape[2:], jnp.int32)

    @pl.when(m == M - 1)
    def _():
        @pl.loop(0, X + 2 * HALO)
        def _(x):
            fe[x, HALO + Y :] = jnp.zeros((HALO,) + fe.shape[2:], F32)

        ae[:, 1 + by :] = jnp.zeros((bx + 2, 1) + ae.shape[2:], jnp.int32)

    def beside(index, count):
        return (index + count - 1) // count + (2 * (count - 1) - index) // count

    pl.semaphore_wait(barrier, beside(g, G) + beside(m, M))

    def copies(ref, h, n, axis, dev, send, recv, down, slot):
        def cut(start, length):
            if axis == 0:
                inner = ref.shape[1] - 2 * h
                return ref.at[pl.ds(start, length), pl.ds(h, inner)]
            return ref.at[:, pl.ds(start, length)]

        src = cut(h, h) if down else cut(n, h)
        dst = cut(n + h, h) if down else cut(0, h)
        return pltpu.make_async_remote_copy(
            src_ref=src,
            dst_ref=dst,
            send_sem=send.at[slot],
            recv_sem=recv.at[slot],
            device_id=dev,
            device_id_type=MESH,
        )

    def phase(axis, name, index, count, send, recv):
        if count == 1:
            return
        lower, upper = {name: index - 1}, {name: index + 1}
        nf, na = (X, bx) if axis == 0 else (Y, by)

        def make(down, dev):
            base = 0 if down else 2
            return (
                copies(fe, HALO, nf, axis, dev, send, recv, down, base),
                copies(ae, 1, na, axis, dev, send, recv, down, base + 1),
            )

        @pl.when(index > 0)
        def _():
            for c in make(True, lower):
                c.start()

        @pl.when(index < count - 1)
        def _():
            for c in make(False, upper):
                c.start()

        @pl.when(index > 0)
        def _():
            for c in make(True, lower):
                c.wait_send()
            for c in make(False, lower):
                c.wait_recv()

        @pl.when(index < count - 1)
        def _():
            for c in make(False, upper):
                c.wait_send()
            for c in make(True, upper):
                c.wait_recv()

    phase(0, "grp", g, G, sx, rx)
    phase(1, "mem", m, M, sy, ry)


def sweep(src, x0, x1, y0, y1, emit):
    Z = src.shape[-1]
    lane = lax.broadcasted_iota(jnp.int32, (src.shape[2], Z), 1)
    first, last = lane == 0, lane == Z - 1

    @pl.loop(x0, x1)
    def _(x):
        prev, here = src[x, y0 - 1], src[x, y0]
        for y in range(y0, y1):
            after = src[x, y + 1]
            near = src[x - 1, y] + src[x + 1, y] + (prev + after)
            low = jnp.where(first, 0.0, pltpu.roll(here, 1, 1))
            high = jnp.where(last, 0.0, pltpu.roll(here, Z - 1, 1))
            emit(x, y, here, near + (low + high))
            prev, here = here, after


def clear_outside(ref, G, M, X, Y, width):
    g, m = lax.axis_index("grp"), lax.axis_index("mem")
    h = HALO
    rest = ref.shape[2:]

    def rows(start):
        @pl.loop(start, start + width)
        def _(x):
            ref[x] = jnp.zeros(ref.shape[1:], F32)

    def columns(start):
        @pl.loop(h - width, h + X + width)
        def _(x):
            ref[x, start : start + width] = jnp.zeros((width,) + rest, F32)

    pl.when(g == 0)(lambda: rows(h - width))
    pl.when(g == G - 1)(lambda: rows(h + X))
    pl.when(m == 0)(lambda: columns(h - width))
    pl.when(m == M - 1)(lambda: columns(h + Y))


def pre_kernel(G, M, chunk, fe, ids_ref, s3, d_ref, s2, means):
    Xe, Ye, K, Z = fe.shape
    X, Y = Xe - 2 * HALO, Ye - 2 * HALO
    bx, by, bz = X // CELL, Y // CELL, Z // CELL
    w = WEIGHT

    def second(x, y, c, near):
        s2[x, y] = w * ((2.0 - 6.0 * w) * c + w * near)

    sweep(fe, 1, Xe - 1, 1, Ye - 1, second)
    clear_outside(s2, G, M, X, Y, 3)

    def third(x, y, c, near):
        s3[x, y] = (1.0 - 6.0 * w) * c + w * (fe[x, y] + near)

    sweep(s2, 2, Xe - 2, 2, Ye - 2, third)
    clear_outside(s3, G, M, X, Y, 2)

    def residual(x, y, c, near):
        s2[x, y] = fe[x, y] - 6.0 * c + near

    sweep(s3, HALO, HALO + X, HALO, HALO + Y, residual)

    rows = lax.broadcasted_iota(jnp.int32, (by * Z, by * bz), 0)
    cols = lax.broadcasted_iota(jnp.int32, (by * Z, by * bz), 1)
    spread = jnp.where(rows // CELL == cols, 1.0 / CELL**3, 0.0).astype(BF16)
    for i in range(bx):
        parts = []
        for j in range(by):
            total = None
            for p in range(CELL):
                for q in range(CELL):
                    v = s2[HALO + i * CELL + p, HALO + j * CELL + q]
                    total = v if total is None else total + v
            parts.append(total)
        line = jnp.concatenate(parts, axis=1)
        means[:, i * by * bz : (i + 1) * by * bz] = joined(
            jnp.dot(pieces(line), spread, preferred_element_type=F32)
        )
    split = pieces(means[...])
    ids = ids_ref[...]
    count = bx * by * bz

    @pl.loop(0, d_ref.shape[0])
    def _(o):
        entry = lax.broadcasted_iota(jnp.int32, (chunk, count), 0) + o * chunk
        hot = jnp.where(entry == ids, 1.0, 0.0).astype(BF16)
        got = lax.dot_general(
            split, hot, (((1,), (1,)), ((), ())), preferred_element_type=F32
        )
        d_ref[o] = joined(got)


def coarse_kernel(G, M, n_own, d_ref, fac_ref, x_ref, r, ssend, srecv, gsend, grecv):
    n = G * M
    owners = n_own * M
    g, m = lax.axis_index("grp"), lax.axis_index("mem")
    me = g * M + m
    own = m * n_own + g
    q, bs = fac_ref.shape[0], fac_ref.shape[1]
    everyone = n_own == G

    def device(i):
        return {"grp": i // M, "mem": i % M}

    def peer(t):
        return lax.rem(me + t, n)

    barrier = pltpu.get_barrier_semaphore()

    @pl.loop(1, n)
    def _(t):
        pl.semaphore_signal(barrier, inc=1, device_id=device(peer(t)), device_id_type=MESH)

    pl.semaphore_wait(barrier, n - 1)

    def owning(i, body):
        if everyone:
            body()
        else:
            pl.when(i // M < n_own)(body)

    @pl.loop(1, n)
    def _(t):
        to = peer(t)

        def go():
            pltpu.make_async_remote_copy(
                src_ref=d_ref.at[(to % M) * n_own + to // M],
                dst_ref=r.at[me],
                send_sem=ssend,
                recv_sem=srecv,
                device_id=device(to),
                device_id_type=MESH,
            ).start()

        owning(to, go)

    def wait_bytes(ref, count, sem):
        if count > 0:
            part = ref.at[pl.ds(0, count)]
            pltpu.make_async_copy(part, part, sem).wait()

    def solve():
        wait_bytes(r, n - 1, srecv)

        def add(t, total):
            return total + r[peer(t)]

        total = lax.fori_loop(1, n, add, d_ref[own])
        for b in range(q):
            rhs = total[:, b * bs : (b + 1) * bs]
            inner = lax.dot_general(
                rhs,
                fac_ref[b],
                (((1,), (1,)), ((), ())),
                precision=lax.Precision.HIGHEST,
                preferred_element_type=F32,
            )
            x_ref[own, :, b * bs : (b + 1) * bs] = lax.dot_general(
                inner,
                fac_ref[b],
                (((1,), (0,)), ((), ())),
                precision=lax.Precision.HIGHEST,
                preferred_element_type=F32,
            )

        @pl.loop(1, n)
        def _(t):
            pltpu.make_async_remote_copy(
                src_ref=x_ref.at[own],
                dst_ref=x_ref.at[own],
                send_sem=gsend,
                recv_sem=grecv,
                device_id=device(peer(t)),
                device_id_type=MESH,
            ).start()

    owning(me, solve)

    if everyone:
        wait_bytes(d_ref, n - 1, ssend)
        wait_bytes(x_ref, n - 1, grecv)
        wait_bytes(r, n - 1, gsend)
    else:
        mine = g < n_own

        @pl.when(mine)
        def _():
            wait_bytes(d_ref, owners - 1, ssend)
            wait_bytes(x_ref, owners - 1, grecv)
            wait_bytes(r, n - 1, gsend)

        @pl.when(jnp.logical_not(mine))
        def _():
            wait_bytes(d_ref, owners, ssend)
            wait_bytes(x_ref, owners, grecv)


def post_kernel(G, M, bs, fe, s3, ae, x_ref, o_ref, lifted, sol):
    Xe, Ye, K, Z = fe.shape
    X, Y = Xe - 2 * HALO, Ye - 2 * HALO
    bx, by, bz = X // CELL + 2, Y // CELL + 2, Z // CELL
    w = WEIGHT
    half = 8
    owners, q = x_ref.shape[0], x_ref.shape[2] // bs
    per = Z // bz
    groups = [range(s, min(s + per, by)) for s in range(0, by, per)]
    lane = lax.broadcasted_iota(jnp.int32, (half, Z), 1)

    def pick(table, index):
        return jnp.take_along_axis(table, index, axis=1)

    def line(i):
        for group in groups:
            index = None
            for slot, j in enumerate(group):
                packed = pick(ae[i, j], (lane % bz) * CELL)
                index = packed if index is None else jnp.where(lane // bz == slot, packed, index)
            inner = index % bs
            outer = index // bs
            found = [jnp.zeros((half, Z), F32) for _ in range(K // half)]

            def body(o, found):
                out = list(found)
                for b in range(q):
                    hit = outer == o * q + b
                    for h in range(K // half):
                        table = x_ref[o, h * half : (h + 1) * half, b * bs : (b + 1) * bs]
                        out[h] = jnp.where(hit, pick(table, inner), out[h])
                return tuple(out)

            found = lax.fori_loop(0, owners, body, tuple(found))
            for slot, j in enumerate(group):
                wide = [pick(v, lane // CELL + slot * bz) for v in found]
                value = jnp.concatenate(wide, axis=0)
                for p in range(CELL):
                    for r in range(CELL):
                        lifted[i * CELL + p, j * CELL + r] = value

    @pl.loop(0, bx)
    def _(i):
        line(i)

    clear_outside(lifted, G, M, X, Y, HALO)

    def start(x, y, c, near):
        sol[x, y] = s3[x, y] + ((1.0 - 6.0 * w) * c + w * near)

    sweep(lifted, 2, Xe - 2, 2, Ye - 2, start)
    clear_outside(sol, G, M, X, Y, 2)

    def first(x, y, c, near):
        lifted[x, y] = (1.0 - 6.0 * w) * c + w * (fe[x, y] + near)

    sweep(sol, 3, Xe - 3, 3, Ye - 3, first)
    clear_outside(lifted, G, M, X, Y, 1)

    flat = o_ref.reshape(K * X * Y, Z)

    def last(x, y, c, near):
        flat[pl.ds((x - HALO) * Y + (y - HALO), K, stride=X * Y), :] = (
            1.0 - 6.0 * w
        ) * c + w * (fe[x, y] + near)

    sweep(lifted, HALO, HALO + X, HALO, HALO + Y, last)


def shards(G, M, forcing, aggregate, factors):
    K, X, Y, Z = forcing.shape
    bx, by, bz = aggregate.shape
    Xe, Ye = X + 2 * HALO, Y + 2 * HALO
    local_blocks, bs = factors.shape[0], factors.shape[1]
    q = -(-local_blocks // G)
    n_own = local_blocks // q
    chunk = q * bs
    owners = n_own * M
    sd = jax.ShapeDtypeStruct

    wide_ids = jnp.broadcast_to(
        jnp.repeat(aggregate, CELL, axis=2)[:, :, None, :], (bx, by, 8, Z)
    )
    fe, ae = pl.pallas_call(
        functools.partial(halo_kernel, G, M),
        out_shape=(sd((Xe, Ye, K, Z), F32), sd((bx + 2, by + 2, 8, Z), jnp.int32)),
        in_specs=[vmem_spec()] * 2,
        out_specs=(vmem_spec(),) * 2,
        scratch_shapes=[pltpu.SemaphoreType.DMA((4,))] * 4,
        compiler_params=params(collective_id=0, has_side_effects=True),
        name="halo",
    )(forcing, wide_ids)

    s3, dense = pl.pallas_call(
        functools.partial(pre_kernel, G, M, chunk),
        out_shape=(sd((Xe, Ye, K, Z), F32), sd((owners, K, chunk), F32)),
        in_specs=[vmem_spec()] * 2,
        out_specs=(vmem_spec(),) * 2,
        scratch_shapes=[VMEM((Xe, Ye, K, Z), F32), VMEM((K, bx * by * bz), F32)],
        compiler_params=params(),
        name="pre",
    )(fe, aggregate.reshape(1, -1))

    g = lax.axis_index("grp")
    mine = lax.dynamic_slice_in_dim(factors, jnp.minimum(g, n_own - 1) * q, q, axis=0)
    fix = pl.pallas_call(
        functools.partial(coarse_kernel, G, M, n_own),
        out_shape=sd((owners, K, chunk), F32),
        in_specs=[vmem_spec()] * 2,
        out_specs=vmem_spec(),
        scratch_shapes=[VMEM((G * M, K, chunk), F32)] + [pltpu.SemaphoreType.DMA] * 4,
        compiler_params=params(collective_id=1, has_side_effects=True),
        name="coarse",
    )(dense, mine)

    return pl.pallas_call(
        functools.partial(post_kernel, G, M, bs),
        out_shape=sd((K, X, Y, Z), F32),
        in_specs=[vmem_spec()] * 4,
        out_specs=vmem_spec(),
        scratch_shapes=[VMEM((Xe, Ye, K, Z), F32)] * 2,
        compiler_params=params(),
        name="post",
    )(fe, s3, ae, fix)


def solution(mesh):
    placed = (P(None, "grp", "mem", None), P("grp", "mem", None), P("mem", None, None))
    body = functools.partial(shards, mesh.shape["grp"], mesh.shape["mem"])
    return jax.shard_map(
        body, mesh=mesh, in_specs=placed, out_specs=P(None, "grp", "mem", None), check_vma=False
    )
```

time: 381 us -> 136 us (0.36)
  waiting for transfers between devices: 221 us -> 0 us
  Pallas kernels: 0 us -> 129 us
  starting transfers between devices: 48.9 us -> 0 us
  local copies, waits for them, and re-layouts: 49.7 us -> 3.9 us
  other arithmetic: 32.7 us -> 0 us
  between operations: 15.5 us -> 0.03 us
  matrix products: 12.4 us -> 0 us
    psum x1 -> x0, waiting for transfers between devices: 167 us -> none  [shards(): coarse_rhs = lax.psum(partial_value, ('grp', 'mem'))]
    pallas_call x0 -> x4, Pallas kernels: none -> 129 us  [the longest x1 44.9 us: shards(): pl.pallas_call(functools.partial(post_kernel, G, M, bs), out_shape=sd((K,...]
    ppermute x24 -> x0, waiting for transfers between devices: 54 us -> none  [the longest x12 27 us: with_halo(): lax.ppermute(tail, axis, [(i, (i + 1) % count) for i in range(ends)])]
    ppermute x24 -> x0, starting transfers between devices: 48.7 us -> none  [the longest x12 26.1 us: with_halo(): lax.ppermute(tail, axis, [(i, (i + 1) % count) for i in range(ends)])]
    reshape x3 -> x1, local copies, waits for them, and re-layouts: 17.1 us -> 1.51 us  [shards(): aggregate.reshape(1, -1)]
    dot_general x2 -> x0, matrix products: 12.4 us -> none  [the longest x1 8.64 us: solve_blocks(): jnp.einsum('kbj,bij->kbi', blocks, factors, precision=lax.Precision.HIGHEST)]
    add x5 -> x0, other arithmetic: 11.1 us -> none  [the longest x2 5.03 us: shards(): solution = solution + weight * (forcing - apply_operator(solution))]
    sub x1 -> x0, local copies, waits for them, and re-layouts: 10 us -> none  [shards(): residual = forcing - apply_operator(smoothed)]
  transfers between devices with their start and end apart: 26 -> 0, of which waited for: 22 -> 0; matrix products, arithmetic and copies ran while one was open for 4% -> 0% of each run, Pallas kernels for 0% -> 0%
where the time goes in v1:
time: 136 us; the launch traced here: 133 us
  Pallas kernels  129 us (95%)
  local copies, waits for them, and re-layouts  3.9 us (3%)
    pallas_call x1, Pallas kernels, shards(): pl.pallas_call(functools.partial(post_kernel, G, M, bs), out_shape=sd((K,...  44.9 us
    pallas_call x1, Pallas kernels, shards(): pl.pallas_call(functools.partial(coarse_kernel, G, M, n_own), out_shape=s...  34.9 us
    pallas_call x1, Pallas kernels, shards(): pl.pallas_call(functools.partial(halo_kernel, G, M), out_shape=(sd((Xe, Y...  29 us
    pallas_call x1, Pallas kernels, shards(): pl.pallas_call(functools.partial(pre_kernel, G, M, chunk), out_shape=(sd(...  20.7 us

profile of v1, /device:TPU:8, one launch (start us, length us, event | category | flops | bytes accessed | tf_op | source)
XLA Modules:
  0.0 133.4 jit_solution(26251890119923266)
XLA Ops:
  0.0 0.0 copy-start
  0.0 1.5 %reshape.4.ids_ref = s32[1,512]{1,0:T(1,128)} reshape(s32[4,4,32]{2,1,0:T(4,128)} %param.4) | data formatting | bytes 4096 | tf_op jit(solution)/shard_map/reshape | solution.py:460
  1.5 0.1 copy-done
  1.6 0.7 constant_dynamic-slice_fusion.fac_ref
  2.3 0.8 broadcast_in_dim.10
  3.1 0.2 broadcast_in_dim.11
  3.3 0.6 broadcast_in_dim.12.a_ref
  3.9 29.0 %halo.1 = (f32[24,24,16,128]{3,2,1,0:T(8,128)}, s32[6,6,8,128]{3,2,1,0:T(8,128)}) custom-call(f32[16,16,16,128]{3,2,1,0:T(8,128)} %f_ref.1, s32[4,4,8,128]{3,2,1,0:T(8,128)} %broadcast_in_dim.12.a_ref), custom_call_target="tpu_custom_call" | custom-call | tf_op jit(solution)/shard_map/halo/pallas_call | solution.py:442
  32.9 20.7 %pre.1 = (f32[24,24,16,128]{3,2,1,0:T(8,128)}, f32[32,16,256]{2,1,0:T(8,128)}) custom-call(f32[24,24,16,128]{3,2,1,0:T(8,128)} %get-tuple-element.9.fe, s32[1,512]{1,0:T(1,128)} %reshape.4.ids_ref), custom_call_target="tpu_custom_call" | custom-call | tf_op jit(solution)/shard_map/pre/pallas_call | solution.py:452
  53.6 34.9 %coarse.1.x_ref = f32[32,16,256]{2,1,0:T(8,128)} custom-call(f32[32,16,256]{2,1,0:T(8,128)} %get-tuple-element.12.d_ref, f32[2,128,128]{2,1,0:T(8,128)} %constant_dynamic-slice_fusion.fac_ref), custom_call_target="tpu_custom_call" | custom-call | tf_op jit(solution)/shard_map/coarse/pallas_call | solution.py:464
  88.5 44.9 %post.1 = f32[16,16,16,128]{3,2,1,0:T(8,128)} custom-call(f32[24,24,16,128]{3,2,1,0:T(8,128)} %get-tuple-element.9.fe, f32[24,24,16,128]{3,2,1,0:T(8,128)} %get-tuple-element.10.s3, s32[6,6,8,128]{3,2,1,0:T(8,128)} %get-tuple-element.11.ae, f32[32,16,256]{2,1,0:T(8,128)} %coarse.1.x_ref), custom_call_target="tpu_custom_call" | custom-call | tf_op jit(solution)/shard_map/post/pallas_call | solution.py:474
Async XLA Ops:
  0.0 1.6 %copy-start = (f32[32,128,128]{2,1,0:T(8,128)S(1)}, f32[32,128,128]{2,1,0:T(8,128)}, u32[]{:S(2)}) copy-start(f32[32,128,128]{2,1,0:T(8,128)} %param.5) | copy-start | bytes 6291460

commit v2 on v1

--- a/solution.py
+++ b/solution.py
@@ -39,7 +39,7 @@
     return value[:k] + (value[k : 2 * k] + value[2 * k :])
 
 
-def halo_kernel(G, M, f_ref, a_ref, fe, ae, sx, rx, sy, ry):
+def halo_kernel(G, M, f_ref, a_ref, fe, ae, sx, rx, sy, ry, sc, rc):
     K, X, Y, Z = f_ref.shape
     bx, by = X // CELL, Y // CELL
     g, m = lax.axis_index("grp"), lax.axis_index("mem")
@@ -100,63 +100,85 @@
 
     pl.semaphore_wait(barrier, beside(g, G) + beside(m, M))
 
-    def copies(ref, h, n, axis, dev, send, recv, down, slot):
-        def cut(start, length):
-            if axis == 0:
-                inner = ref.shape[1] - 2 * h
-                return ref.at[pl.ds(start, length), pl.ds(h, inner)]
-            return ref.at[:, pl.ds(start, length)]
-
-        src = cut(h, h) if down else cut(n, h)
-        dst = cut(n + h, h) if down else cut(0, h)
+    def copy(ref, src, dst, dev, sems, slot):
         return pltpu.make_async_remote_copy(
-            src_ref=src,
-            dst_ref=dst,
-            send_sem=send.at[slot],
-            recv_sem=recv.at[slot],
+            src_ref=ref.at[src],
+            dst_ref=ref.at[dst],
+            send_sem=sems[0].at[slot],
+            recv_sem=sems[1].at[slot],
             device_id=dev,
             device_id_type=MESH,
         )
 
-    def phase(axis, name, index, count, send, recv):
-        if count == 1:
-            return
-        lower, upper = {name: index - 1}, {name: index + 1}
-        nf, na = (X, bx) if axis == 0 else (Y, by)
-
-        def make(down, dev):
-            base = 0 if down else 2
-            return (
-                copies(fe, HALO, nf, axis, dev, send, recv, down, base),
-                copies(ae, 1, na, axis, dev, send, recv, down, base + 1),
-            )
-
-        @pl.when(index > 0)
-        def _():
-            for c in make(True, lower):
+    def faces(down, axis, dev):
+        out = []
+        n, other = ((X, Y), (Y, X))[axis]
+        nb, otherb = ((bx, by), (by, bx))[axis]
+        for slot, (ref, h, length, across) in enumerate(
+            ((fe, HALO, n, other), (ae, 1, nb, otherb))
+        ):
+            src = pl.ds(h if down else length, h)
+            dst = pl.ds(length + h if down else 0, h)
+            whole = pl.ds(h, across)
+            pick = (lambda d: (d, whole)) if axis == 0 else (lambda d: (whole, d))
+            base = (0 if down else 2) + slot
+            out.append(copy(ref, pick(src), pick(dst), dev, (sx, rx) if axis == 0 else (sy, ry), base))
+        return out
+
+    def corners(down, dev):
+        out = []
+        slot = 0 if down else 2 * HALO
+        for d in range(1, HALO):
+            width = HALO - d
+            src = pl.ds(HALO if down else HALO + Y - width, width)
+            dst = pl.ds(HALO + Y if down else HALO - width, width)
+            for row in (HALO - d, HALO + X - 1 + d):
+                out.append(copy(fe, (row, src), (row, dst), dev, (sc, rc), slot))
+                slot += 1
+        src = pl.ds(1 if down else by, 1)
+        dst = pl.ds(1 + by if down else 0, 1)
+        for row in (0, bx + 1):
+            out.append(copy(ae, (row, src), (row, dst), dev, (sc, rc), slot))
+            slot += 1
+        return out
+
+    def each(index, count, name, body):
+        if count > 1:
+            pl.when(index > 0)(lambda: body(True, {name: index - 1}))
+            pl.when(index < count - 1)(lambda: body(False, {name: index + 1}))
+
+    def start_faces(axis):
+        def body(down, dev):
+            for c in faces(down, axis, dev):
                 c.start()
 
-        @pl.when(index < count - 1)
-        def _():
-            for c in make(False, upper):
-                c.start()
-
-        @pl.when(index > 0)
-        def _():
-            for c in make(True, lower):
+        return body
+
+    def end_faces(axis):
+        def body(down, dev):
+            for c in faces(down, axis, dev):
                 c.wait_send()
-            for c in make(False, lower):
+            for c in faces(not down, axis, dev):
                 c.wait_recv()
 
-        @pl.when(index < count - 1)
-        def _():
-            for c in make(False, upper):
-                c.wait_send()
-            for c in make(True, upper):
-                c.wait_recv()
-
-    phase(0, "grp", g, G, sx, rx)
-    phase(1, "mem", m, M, sy, ry)
+        return body
+
+    def start_corners(down, dev):
+        for c in corners(down, dev):
+            c.start()
+
+    def end_corners(down, dev):
+        for c in corners(down, dev):
+            c.wait_send()
+        for c in corners(not down, dev):
+            c.wait_recv()
+
+    each(g, G, "grp", start_faces(0))
+    each(m, M, "mem", start_faces(1))
+    each(g, G, "grp", end_faces(0))
+    each(m, M, "mem", start_corners)
+    each(m, M, "mem", end_faces(1))
+    each(m, M, "mem", end_corners)
 
 
 def sweep(src, x0, x1, y0, y1, emit):
@@ -197,7 +219,7 @@
     pl.when(m == M - 1)(lambda: columns(h + Y))
 
 
-def pre_kernel(G, M, chunk, fe, ids_ref, s3, d_ref, s2, means):
+def pre_kernel(G, M, chunk, side, fe, ids_ref, s3, d_ref, s2, means):
     Xe, Ye, K, Z = fe.shape
     X, Y = Xe - 2 * HALO, Ye - 2 * HALO
     bx, by, bz = X // CELL, Y // CELL, Z // CELL
@@ -240,60 +262,72 @@
     ids = ids_ref[...]
     count = bx * by * bz
 
-    @pl.loop(0, d_ref.shape[0])
-    def _(o):
-        entry = lax.broadcasted_iota(jnp.int32, (chunk, count), 0) + o * chunk
-        hot = jnp.where(entry == ids, 1.0, 0.0).astype(BF16)
-        got = lax.dot_general(
-            split, hot, (((1,), (1,)), ((), ())), preferred_element_type=F32
-        )
-        d_ref[o] = joined(got)
-
-
-def coarse_kernel(G, M, n_own, d_ref, fac_ref, x_ref, r, ssend, srecv, gsend, grecv):
-    n = G * M
-    owners = n_own * M
+    entry = lax.broadcasted_iota(jnp.int32, (chunk, count), 0)
+
+    @pl.loop(0, d_ref.shape[1])
+    def _(h):
+        for c in range(2):
+            owner = (h // side) * 2 * side + 2 * (h % side) + c
+            hot = jnp.where(entry == ids - owner * chunk, 1.0, 0.0).astype(BF16)
+            got = lax.dot_general(
+                split, hot, (((1,), (1,)), ((), ())), preferred_element_type=F32
+            )
+            d_ref[c, h] = joined(got)
+
+
+def coarse_kernel(
+    G, M, n_own, d_ref, fac_ref, x_ref, r, pair, e, psend, precv, ssend, srecv, gsend, grecv, fsend, frecv
+):
+    n = G * M // 2
+    side = n_own // 2
+    held = side * M
     g, m = lax.axis_index("grp"), lax.axis_index("mem")
-    me = g * M + m
-    own = m * n_own + g
+    core = lax.rem(g, 2)
+    me = (g // 2) * M + m
+    own = m * side + g // 2
     q, bs = fac_ref.shape[0], fac_ref.shape[1]
     everyone = n_own == G
+    partner = {"grp": g + 1 - 2 * core, "mem": m}
 
     def device(i):
-        return {"grp": i // M, "mem": i % M}
+        return {"grp": 2 * (i // M) + core, "mem": i % M}
 
     def peer(t):
         return lax.rem(me + t, n)
 
+    def send(src, dst, ssem, rsem, to):
+        return pltpu.make_async_remote_copy(
+            src_ref=src, dst_ref=dst, send_sem=ssem, recv_sem=rsem, device_id=to, device_id_type=MESH
+        )
+
     barrier = pltpu.get_barrier_semaphore()
+    pl.semaphore_signal(barrier, inc=1, device_id=partner, device_id_type=MESH)
 
     @pl.loop(1, n)
     def _(t):
         pl.semaphore_signal(barrier, inc=1, device_id=device(peer(t)), device_id_type=MESH)
 
-    pl.semaphore_wait(barrier, n - 1)
+    pl.semaphore_wait(barrier, n)
 
     def owning(i, body):
         if everyone:
             body()
         else:
-            pl.when(i // M < n_own)(body)
+            pl.when(i // M < side)(body)
+
+    swap = send(d_ref.at[1 - core], pair, psend, precv, partner)
+    swap.start()
+    swap.wait()
+
+    @pl.loop(0, held)
+    def _(h):
+        e[h] = d_ref[core, h] + pair[h]
 
     @pl.loop(1, n)
     def _(t):
         to = peer(t)
-
-        def go():
-            pltpu.make_async_remote_copy(
-                src_ref=d_ref.at[(to % M) * n_own + to // M],
-                dst_ref=r.at[me],
-                send_sem=ssend,
-                recv_sem=srecv,
-                device_id=device(to),
-                device_id_type=MESH,
-            ).start()
-
-        owning(to, go)
+        block = (to % M) * side + to // M
+        owning(to, lambda: send(e.at[block], r.at[me], ssend, srecv, device(to)).start())
 
     def wait_bytes(ref, count, sem):
         if count > 0:
@@ -306,7 +340,7 @@
         def add(t, total):
             return total + r[peer(t)]
 
-        total = lax.fori_loop(1, n, add, d_ref[own])
+        total = lax.fori_loop(1, n, add, e[own])
         for b in range(q):
             rhs = total[:, b * bs : (b + 1) * bs]
             inner = lax.dot_general(
@@ -316,7 +350,7 @@
                 precision=lax.Precision.HIGHEST,
                 preferred_element_type=F32,
             )
-            x_ref[own, :, b * bs : (b + 1) * bs] = lax.dot_general(
+            x_ref[core, own, :, b * bs : (b + 1) * bs] = lax.dot_general(
                 inner,
                 fac_ref[b],
                 (((1,), (0,)), ((), ())),
@@ -326,43 +360,41 @@
 
         @pl.loop(1, n)
         def _(t):
-            pltpu.make_async_remote_copy(
-                src_ref=x_ref.at[own],
-                dst_ref=x_ref.at[own],
-                send_sem=gsend,
-                recv_sem=grecv,
-                device_id=device(peer(t)),
-                device_id_type=MESH,
-            ).start()
+            mine = x_ref.at[core, own]
+            send(mine, mine, gsend, grecv, device(peer(t))).start()
 
     owning(me, solve)
 
     if everyone:
-        wait_bytes(d_ref, n - 1, ssend)
-        wait_bytes(x_ref, n - 1, grecv)
+        wait_bytes(e, held - 1, ssend)
+        wait_bytes(e, held - 1, grecv)
         wait_bytes(r, n - 1, gsend)
     else:
         mine = g < n_own
 
         @pl.when(mine)
         def _():
-            wait_bytes(d_ref, owners - 1, ssend)
-            wait_bytes(x_ref, owners - 1, grecv)
+            wait_bytes(e, held - 1, ssend)
+            wait_bytes(e, held - 1, grecv)
             wait_bytes(r, n - 1, gsend)
 
         @pl.when(jnp.logical_not(mine))
         def _():
-            wait_bytes(d_ref, owners, ssend)
-            wait_bytes(x_ref, owners, grecv)
-
-
-def post_kernel(G, M, bs, fe, s3, ae, x_ref, o_ref, lifted, sol):
+            wait_bytes(e, held, ssend)
+            wait_bytes(e, held, grecv)
+
+    forward = send(x_ref.at[core], x_ref.at[core], fsend, frecv, partner)
+    forward.start()
+    forward.wait()
+
+
+def post_kernel(G, M, bs, side, fe, s3, ae, x_ref, o_ref, lifted, sol):
     Xe, Ye, K, Z = fe.shape
     X, Y = Xe - 2 * HALO, Ye - 2 * HALO
     bx, by, bz = X // CELL + 2, Y // CELL + 2, Z // CELL
     w = WEIGHT
     half = 8
-    owners, q = x_ref.shape[0], x_ref.shape[2] // bs
+    q = x_ref.shape[3] // bs
     per = Z // bz
     groups = [range(s, min(s + per, by)) for s in range(0, by, per)]
     lane = lax.broadcasted_iota(jnp.int32, (half, Z), 1)
@@ -370,36 +402,51 @@
     def pick(table, index):
         return jnp.take_along_axis(table, index, axis=1)
 
-    def line(i):
-        for group in groups:
+    def lines(base, count):
+        rows = [(base + d, group) for d in range(count) for group in groups]
+        inner, outer = [], []
+        for i, group in rows:
             index = None
             for slot, j in enumerate(group):
                 packed = pick(ae[i, j], (lane % bz) * CELL)
                 index = packed if index is None else jnp.where(lane // bz == slot, packed, index)
-            inner = index % bs
-            outer = index // bs
-            found = [jnp.zeros((half, Z), F32) for _ in range(K // half)]
-
-            def body(o, found):
-                out = list(found)
+            inner.append(index % bs)
+            outer.append(index // bs)
+        halves = K // half
+
+        def body(h, found):
+            out = list(found)
+            for c in range(2):
+                owner = (h // side) * 2 * side + 2 * (h % side) + c
                 for b in range(q):
-                    hit = outer == o * q + b
-                    for h in range(K // half):
-                        table = x_ref[o, h * half : (h + 1) * half, b * bs : (b + 1) * bs]
-                        out[h] = jnp.where(hit, pick(table, inner), out[h])
-                return tuple(out)
-
-            found = lax.fori_loop(0, owners, body, tuple(found))
+                    tables = [
+                        x_ref[c, h, t * half : (t + 1) * half, b * bs : (b + 1) * bs]
+                        for t in range(halves)
+                    ]
+                    for e in range(len(rows)):
+                        hit = outer[e] == owner * q + b
+                        for t in range(halves):
+                            k = e * halves + t
+                            out[k] = jnp.where(hit, pick(tables[t], inner[e]), out[k])
+            return tuple(out)
+
+        zeros = tuple(jnp.zeros((half, Z), F32) for _ in range(len(rows) * halves))
+        found = lax.fori_loop(0, x_ref.shape[1], body, zeros)
+        for e, (i, group) in enumerate(rows):
             for slot, j in enumerate(group):
-                wide = [pick(v, lane // CELL + slot * bz) for v in found]
+                wide = [
+                    pick(found[e * halves + t], lane // CELL + slot * bz) for t in range(halves)
+                ]
                 value = jnp.concatenate(wide, axis=0)
                 for p in range(CELL):
                     for r in range(CELL):
                         lifted[i * CELL + p, j * CELL + r] = value
 
-    @pl.loop(0, bx)
+    batch = max(d for d in (1, 2, 3) if bx % d == 0)
+
+    @pl.loop(0, bx // batch)
     def _(i):
-        line(i)
+        lines(i * batch, batch)
 
     clear_outside(lifted, G, M, X, Y, HALO)
 
@@ -444,14 +491,15 @@
         out_shape=(sd((Xe, Ye, K, Z), F32), sd((bx + 2, by + 2, 8, Z), jnp.int32)),
         in_specs=[vmem_spec()] * 2,
         out_specs=(vmem_spec(),) * 2,
-        scratch_shapes=[pltpu.SemaphoreType.DMA((4,))] * 4,
+        scratch_shapes=[pltpu.SemaphoreType.DMA((4,))] * 4
+        + [pltpu.SemaphoreType.DMA((4 * HALO,))] * 2,
         compiler_params=params(collective_id=0, has_side_effects=True),
         name="halo",
     )(forcing, wide_ids)
 
     s3, dense = pl.pallas_call(
-        functools.partial(pre_kernel, G, M, chunk),
-        out_shape=(sd((Xe, Ye, K, Z), F32), sd((owners, K, chunk), F32)),
+        functools.partial(pre_kernel, G, M, chunk, n_own // 2),
+        out_shape=(sd((Xe, Ye, K, Z), F32), sd((2, owners // 2, K, chunk), F32)),
         in_specs=[vmem_spec()] * 2,
         out_specs=(vmem_spec(),) * 2,
         scratch_shapes=[VMEM((Xe, Ye, K, Z), F32), VMEM((K, bx * by * bz), F32)],
@@ -463,16 +511,16 @@
     mine = lax.dynamic_slice_in_dim(factors, jnp.minimum(g, n_own - 1) * q, q, axis=0)
     fix = pl.pallas_call(
         functools.partial(coarse_kernel, G, M, n_own),
-        out_shape=sd((owners, K, chunk), F32),
+        out_shape=sd((2, owners // 2, K, chunk), F32),
         in_specs=[vmem_spec()] * 2,
         out_specs=vmem_spec(),
-        scratch_shapes=[VMEM((G * M, K, chunk), F32)] + [pltpu.SemaphoreType.DMA] * 4,
+        scratch_shapes=[VMEM((G * M // 2, K, chunk), F32)] + [VMEM((owners // 2, K, chunk), F32)] * 2 + [pltpu.SemaphoreType.DMA] * 8,
         compiler_params=params(collective_id=1, has_side_effects=True),
         name="coarse",
     )(dense, mine)
 
     return pl.pallas_call(
-        functools.partial(post_kernel, G, M, bs),
+        functools.partial(post_kernel, G, M, bs, n_own // 2),
         out_shape=sd((K, X, Y, Z), F32),
         in_specs=[vmem_spec()] * 4,
         out_specs=vmem_spec(),

time: 136 us -> 90.8 us (0.67)
  Pallas kernels: 129 us -> 85.4 us
    pallas_call x2, Pallas kernels: 65.6 us -> 39.5 us  [the longest x1 21 us: shards(): pl.pallas_call(functools.partial(post_kernel, G, M, bs, n_own // 2), out_...]
    pallas_call x1, Pallas kernels: 34.9 us -> 25 us  [shards(): pl.pallas_call(functools.partial(coarse_kernel, G, M, n_own), out_shape=s...]
    pallas_call x1, Pallas kernels: 29 us -> 20.9 us  [shards(): pl.pallas_call(functools.partial(halo_kernel, G, M), out_shape=(sd((Xe, Y...]
where the time goes in v2:
time: 90.8 us; the launch traced here: 89.3 us
  Pallas kernels  85.4 us (94%)
  local copies, waits for them, and re-layouts  3.9 us (4%)
    pallas_call x1, Pallas kernels, shards(): pl.pallas_call(functools.partial(coarse_kernel, G, M, n_own), out_shape=s...  25 us
    pallas_call x1, Pallas kernels, shards(): pl.pallas_call(functools.partial(post_kernel, G, M, bs, n_own // 2), out_...  21 us
    pallas_call x1, Pallas kernels, shards(): pl.pallas_call(functools.partial(halo_kernel, G, M), out_shape=(sd((Xe, Y...  20.9 us
    pallas_call x1, Pallas kernels, shards(): pl.pallas_call(functools.partial(pre_kernel, G, M, chunk, n_own // 2), ou...  18.5 us

profile of v2, /device:TPU:8, one launch (start us, length us, event | category | flops | bytes accessed | tf_op | source)
XLA Modules:
  0.0 89.3 jit_solution(16228164487930469641)
XLA Ops:
  0.0 0.0 copy-start
  0.0 1.5 %reshape.4.ids_ref = s32[1,512]{1,0:T(1,128)} reshape(s32[4,4,32]{2,1,0:T(4,128)} %param.4) | data formatting | bytes 4096 | tf_op jit(solution)/shard_map/reshape | solution.py:508
  1.5 0.1 copy-done
  1.6 0.7 constant_dynamic-slice_fusion.fac_ref
  2.3 0.8 broadcast_in_dim.10
  3.1 0.2 broadcast_in_dim.11
  3.3 0.6 broadcast_in_dim.12.a_ref
  3.9 20.9 %halo.1 = (f32[24,24,16,128]{3,2,1,0:T(8,128)}, s32[6,6,8,128]{3,2,1,0:T(8,128)}) custom-call(f32[16,16,16,128]{3,2,1,0:T(8,128)} %f_ref.1, s32[4,4,8,128]{3,2,1,0:T(8,128)} %broadcast_in_dim.12.a_ref), custom_call_target="tpu_custom_call" | custom-call | tf_op jit(solution)/shard_map/halo/pallas_call | solution.py:489
  24.8 18.5 %pre.1 = (f32[24,24,16,128]{3,2,1,0:T(8,128)}, f32[2,16,16,256]{3,2,1,0:T(8,128)}) custom-call(f32[24,24,16,128]{3,2,1,0:T(8,128)} %get-tuple-element.9.fe, s32[1,512]{1,0:T(1,128)} %reshape.4.ids_ref), custom_call_target="tpu_custom_call" | custom-call | tf_op jit(solution)/shard_map/pre/pallas_call | solution.py:500
  43.3 25.0 %coarse.1.x_ref = f32[2,16,16,256]{3,2,1,0:T(8,128)} custom-call(f32[2,16,16,256]{3,2,1,0:T(8,128)} %get-tuple-element.12.d_ref, f32[2,128,128]{2,1,0:T(8,128)} %constant_dynamic-slice_fusion.fac_ref), custom_call_target="tpu_custom_call" | custom-call | tf_op jit(solution)/shard_map/coarse/pallas_call | solution.py:512
  68.3 21.0 %post.1 = f32[16,16,16,128]{3,2,1,0:T(8,128)} custom-call(f32[24,24,16,128]{3,2,1,0:T(8,128)} %get-tuple-element.9.fe, f32[24,24,16,128]{3,2,1,0:T(8,128)} %get-tuple-element.10.s3, s32[6,6,8,128]{3,2,1,0:T(8,128)} %get-tuple-element.11.ae, f32[2,16,16,256]{3,2,1,0:T(8,128)} %coarse.1.x_ref), custom_call_target="tpu_custom_call" | custom-call | tf_op jit(solution)/shard_map/post/pallas_call | solution.py:522
Async XLA Ops:
  0.0 1.6 %copy-start = (f32[32,128,128]{2,1,0:T(8,128)S(1)}, f32[32,128,128]{2,1,0:T(8,128)}, u32[]{:S(2)}) copy-start(f32[32,128,128]{2,1,0:T(8,128)} %param.5) | copy-start | bytes 6291460

commit v3 on v2

--- a/solution.py
+++ b/solution.py
@@ -22,6 +22,10 @@
     return pl.BlockSpec(memory_space=pltpu.VMEM)
 
 
+def any_spec():
+    return pl.BlockSpec(memory_space=pl.ANY)
+
+
 def params(**kw):
     return pltpu.CompilerParams(vmem_limit_bytes=60 * 1024 * 1024, **kw)
 
@@ -39,36 +43,115 @@
     return value[:k] + (value[k : 2 * k] + value[2 * k :])
 
 
-def halo_kernel(G, M, f_ref, a_ref, fe, ae, sx, rx, sy, ry, sc, rc):
+def sweep(src, x0, x1, y0, y1, emit):
+    Z = src.shape[-1]
+    lane = lax.broadcasted_iota(jnp.int32, (src.shape[2], Z), 1)
+    first, last = lane == 0, lane == Z - 1
+
+    @pl.loop(x0, x1)
+    def _(x):
+        prev, here = src[x, y0 - 1], src[x, y0]
+        for y in range(y0, y1):
+            after = src[x, y + 1]
+            near = src[x - 1, y] + src[x + 1, y] + (prev + after)
+            low = jnp.where(first, 0.0, pltpu.roll(here, 1, 1))
+            high = jnp.where(last, 0.0, pltpu.roll(here, Z - 1, 1))
+            emit(x, y, here, near + (low + high))
+            prev, here = here, after
+
+
+def clear_outside(ref, G, M, X, Y, width):
+    g, m = lax.axis_index("grp"), lax.axis_index("mem")
+    h = HALO
+    rest = ref.shape[2:]
+
+    def rows(start):
+        @pl.loop(start, start + width)
+        def _(x):
+            ref[x] = jnp.zeros(ref.shape[1:], F32)
+
+    def columns(start):
+        @pl.loop(h - width, h + X + width)
+        def _(x):
+            ref[x, start : start + width] = jnp.zeros((width,) + rest, F32)
+
+    pl.when(g == 0)(lambda: rows(h - width))
+    pl.when(g == G - 1)(lambda: rows(h + X))
+    pl.when(m == 0)(lambda: columns(h - width))
+    pl.when(m == M - 1)(lambda: columns(h + Y))
+
+
+def down_kernel(
+    G, M, n_own, f_ref, a_ref, fac_hbm, fe_out, s3_out, ae, x_ref,
+    fe, s3, s2, means, hot, d_ref, r, pair, e, fac_ref,
+    sx, rx, sy, ry, sc, rc, local, psend, precv, ssend, srecv, gsend, grecv, fsend, frecv,
+):
     K, X, Y, Z = f_ref.shape
-    bx, by = X // CELL, Y // CELL
+    Xe, Ye = X + 2 * HALO, Y + 2 * HALO
+    bx, by, bz = a_ref.shape
+    w = WEIGHT
+    n = G * M // 2
+    side = n_own // 2
+    held = side * M
     g, m = lax.axis_index("grp"), lax.axis_index("mem")
+    core = lax.rem(g, 2)
+    me = (g // 2) * M + m
+    own = m * side + g // 2
+    q, bs = fac_ref.shape[0], fac_ref.shape[1]
+    chunk = q * bs
+    everyone = n_own == G
+    partner = {"grp": g + 1 - 2 * core, "mem": m}
     flat = f_ref.reshape(K * X * Y, Z)
 
-    sides = []
-    if G > 1:
-        sides += [(g > 0, {"grp": g - 1}), (g < G - 1, {"grp": g + 1})]
-    if M > 1:
-        sides += [(m > 0, {"mem": m - 1}), (m < M - 1, {"mem": m + 1})]
+    def device(i):
+        return {"grp": 2 * (i // M) + core, "mem": i % M}
+
+    def peer(t):
+        return lax.rem(me + t, n)
+
+    def send(src, dst, ssem, rsem, to):
+        return pltpu.make_async_remote_copy(
+            src_ref=src, dst_ref=dst, send_sem=ssem, recv_sem=rsem, device_id=to, device_id_type=MESH
+        )
+
     barrier = pltpu.get_barrier_semaphore()
-    for there, dev in sides:
-
-        @pl.when(there)
-        def _(dev=dev):
-            pl.semaphore_signal(barrier, inc=1, device_id=dev, device_id_type=MESH)
+
+    def greet(to):
+        pl.semaphore_signal(barrier, inc=1, device_id=to, device_id_type=MESH)
+
+    greet(partner)
+    pl.when(jnp.logical_and(core == 0, g > 0))(lambda: greet({"grp": g - 1, "mem": m}))
+    pl.when(jnp.logical_and(core == 1, g < G - 1))(lambda: greet({"grp": g + 1, "mem": m}))
+
+    @pl.loop(1, n)
+    def _(t):
+        greet(device(peer(t)))
+
+    first = lax.rem(g, n_own) * q
+    fetch = pltpu.make_async_copy(fac_hbm.at[pl.ds(first, q)], fac_ref, local.at[0])
+    fetch.start()
 
     @pl.loop(0, X)
     def _(x):
         for y in range(Y):
             fe[HALO + x, HALO + y] = flat[pl.ds(x * Y + y, K, stride=X * Y), :]
 
-    ae[1 : 1 + bx, 1 : 1 + by] = a_ref[...]
+    for i in range(bx):
+        for j in range(by):
+            row = a_ref[i, j : j + 1, :]
+            wide = jnp.concatenate([row] * (Z // bz), axis=1)
+            ae[1 + i, 1 + j] = jnp.broadcast_to(wide, ae.shape[2:])
 
     def blank(start):
         @pl.loop(start, start + HALO)
         def _(x):
             fe[x, HALO : HALO + Y] = jnp.zeros((Y,) + fe.shape[2:], F32)
 
+    def blank_side(start):
+        @pl.loop(0, Xe)
+        def _(x):
+            fe[x, start : start + HALO] = jnp.zeros((HALO,) + fe.shape[2:], F32)
+
     @pl.when(g == 0)
     def _():
         blank(0)
@@ -81,24 +164,15 @@
 
     @pl.when(m == 0)
     def _():
-        @pl.loop(0, X + 2 * HALO)
-        def _(x):
-            fe[x, 0:HALO] = jnp.zeros((HALO,) + fe.shape[2:], F32)
-
+        blank_side(0)
         ae[:, 0:1] = jnp.zeros((bx + 2, 1) + ae.shape[2:], jnp.int32)
 
     @pl.when(m == M - 1)
     def _():
-        @pl.loop(0, X + 2 * HALO)
-        def _(x):
-            fe[x, HALO + Y :] = jnp.zeros((HALO,) + fe.shape[2:], F32)
-
+        blank_side(HALO + Y)
         ae[:, 1 + by :] = jnp.zeros((bx + 2, 1) + ae.shape[2:], jnp.int32)
 
-    def beside(index, count):
-        return (index + count - 1) // count + (2 * (count - 1) - index) // count
-
-    pl.semaphore_wait(barrier, beside(g, G) + beside(m, M))
+    pl.semaphore_wait(barrier, n + (g + G - 1) // G + (2 * (G - 1) - g) // G - 1)
 
     def copy(ref, src, dst, dev, sems, slot):
         return pltpu.make_async_remote_copy(
@@ -175,72 +249,62 @@
 
     each(g, G, "grp", start_faces(0))
     each(m, M, "mem", start_faces(1))
+
+
+    def second(x, y, c, near):
+        s2[x, y] = w * ((2.0 - 6.0 * w) * c + w * near)
+
+    def third(x, y, c, near):
+        s3[x, y] = (1.0 - 6.0 * w) * c + w * (fe[x, y] + near)
+
+    def residual(x, y, c, near):
+        s2[x, y] = fe[x, y] - 6.0 * c + near
+
+    def inner(src, depth, emit):
+        lo = HALO + depth
+        sweep(src, lo, HALO + X - depth, lo, HALO + Y - depth, emit)
+
+    def ring(src, depth, reach, emit):
+        lo, hx, hy = HALO + depth, HALO + X - depth, HALO + Y - depth
+        y0, y1 = HALO - reach, HALO + Y + reach
+        sweep(src, HALO - reach, lo, y0, y1, emit)
+        sweep(src, hx, HALO + X + reach, y0, y1, emit)
+        sweep(src, lo, hx, y0, lo, emit)
+        sweep(src, lo, hx, hy, y1, emit)
+
+    inner(fe, 1, second)
+    inner(s2, 2, third)
+
+    count = bx * by * bz
+    ids = jnp.concatenate(
+        [a_ref[i, j : j + 1, :] for i in range(bx) for j in range(by)], axis=1
+    )
+    entry = lax.broadcasted_iota(jnp.int32, (chunk, count), 0)
+
+    def owner_of(c, h):
+        return (h // side) * 2 * side + 2 * (h % side) + c
+
+    @pl.loop(0, held)
+    def _(h):
+        for c in range(2):
+            hit = entry == ids - owner_of(c, h) * chunk
+            hot[c, h] = jnp.where(hit, 1.0, 0.0).astype(BF16)
+
     each(g, G, "grp", end_faces(0))
     each(m, M, "mem", start_corners)
     each(m, M, "mem", end_faces(1))
     each(m, M, "mem", end_corners)
 
-
-def sweep(src, x0, x1, y0, y1, emit):
-    Z = src.shape[-1]
-    lane = lax.broadcasted_iota(jnp.int32, (src.shape[2], Z), 1)
-    first, last = lane == 0, lane == Z - 1
-
-    @pl.loop(x0, x1)
-    def _(x):
-        prev, here = src[x, y0 - 1], src[x, y0]
-        for y in range(y0, y1):
-            after = src[x, y + 1]
-            near = src[x - 1, y] + src[x + 1, y] + (prev + after)
-            low = jnp.where(first, 0.0, pltpu.roll(here, 1, 1))
-            high = jnp.where(last, 0.0, pltpu.roll(here, Z - 1, 1))
-            emit(x, y, here, near + (low + high))
-            prev, here = here, after
-
-
-def clear_outside(ref, G, M, X, Y, width):
-    g, m = lax.axis_index("grp"), lax.axis_index("mem")
-    h = HALO
-    rest = ref.shape[2:]
-
-    def rows(start):
-        @pl.loop(start, start + width)
-        def _(x):
-            ref[x] = jnp.zeros(ref.shape[1:], F32)
-
-    def columns(start):
-        @pl.loop(h - width, h + X + width)
-        def _(x):
-            ref[x, start : start + width] = jnp.zeros((width,) + rest, F32)
-
-    pl.when(g == 0)(lambda: rows(h - width))
-    pl.when(g == G - 1)(lambda: rows(h + X))
-    pl.when(m == 0)(lambda: columns(h - width))
-    pl.when(m == M - 1)(lambda: columns(h + Y))
-
-
-def pre_kernel(G, M, chunk, side, fe, ids_ref, s3, d_ref, s2, means):
-    Xe, Ye, K, Z = fe.shape
-    X, Y = Xe - 2 * HALO, Ye - 2 * HALO
-    bx, by, bz = X // CELL, Y // CELL, Z // CELL
-    w = WEIGHT
-
-    def second(x, y, c, near):
-        s2[x, y] = w * ((2.0 - 6.0 * w) * c + w * near)
-
-    sweep(fe, 1, Xe - 1, 1, Ye - 1, second)
+    fe_copy = pltpu.make_async_copy(fe, fe_out, local.at[1])
+    fe_copy.start()
+
+    ring(fe, 1, 3, second)
     clear_outside(s2, G, M, X, Y, 3)
-
-    def third(x, y, c, near):
-        s3[x, y] = (1.0 - 6.0 * w) * c + w * (fe[x, y] + near)
-
-    sweep(s2, 2, Xe - 2, 2, Ye - 2, third)
+    ring(s2, 2, 2, third)
     clear_outside(s3, G, M, X, Y, 2)
-
-    def residual(x, y, c, near):
-        s2[x, y] = fe[x, y] - 6.0 * c + near
-
-    sweep(s3, HALO, HALO + X, HALO, HALO + Y, residual)
+    s3_copy = pltpu.make_async_copy(s3, s3_out, local.at[2])
+    s3_copy.start()
+    inner(s3, 0, residual)
 
     rows = lax.broadcasted_iota(jnp.int32, (by * Z, by * bz), 0)
     cols = lax.broadcasted_iota(jnp.int32, (by * Z, by * bz), 1)
@@ -250,8 +314,8 @@
         for j in range(by):
             total = None
             for p in range(CELL):
-                for q in range(CELL):
-                    v = s2[HALO + i * CELL + p, HALO + j * CELL + q]
+                for t in range(CELL):
+                    v = s2[HALO + i * CELL + p, HALO + j * CELL + t]
                     total = v if total is None else total + v
             parts.append(total)
         line = jnp.concatenate(parts, axis=1)
@@ -259,56 +323,16 @@
             jnp.dot(pieces(line), spread, preferred_element_type=F32)
         )
     split = pieces(means[...])
-    ids = ids_ref[...]
-    count = bx * by * bz
-
-    entry = lax.broadcasted_iota(jnp.int32, (chunk, count), 0)
-
-    @pl.loop(0, d_ref.shape[1])
-    def _(h):
-        for c in range(2):
-            owner = (h // side) * 2 * side + 2 * (h % side) + c
-            hot = jnp.where(entry == ids - owner * chunk, 1.0, 0.0).astype(BF16)
+
+    def scatter(c):
+        @pl.loop(0, held)
+        def _(h):
             got = lax.dot_general(
-                split, hot, (((1,), (1,)), ((), ())), preferred_element_type=F32
+                split, hot[c, h], (((1,), (1,)), ((), ())), preferred_element_type=F32
             )
             d_ref[c, h] = joined(got)
 
-
-def coarse_kernel(
-    G, M, n_own, d_ref, fac_ref, x_ref, r, pair, e, psend, precv, ssend, srecv, gsend, grecv, fsend, frecv
-):
-    n = G * M // 2
-    side = n_own // 2
-    held = side * M
-    g, m = lax.axis_index("grp"), lax.axis_index("mem")
-    core = lax.rem(g, 2)
-    me = (g // 2) * M + m
-    own = m * side + g // 2
-    q, bs = fac_ref.shape[0], fac_ref.shape[1]
-    everyone = n_own == G
-    partner = {"grp": g + 1 - 2 * core, "mem": m}
-
-    def device(i):
-        return {"grp": 2 * (i // M) + core, "mem": i % M}
-
-    def peer(t):
-        return lax.rem(me + t, n)
-
-    def send(src, dst, ssem, rsem, to):
-        return pltpu.make_async_remote_copy(
-            src_ref=src, dst_ref=dst, send_sem=ssem, recv_sem=rsem, device_id=to, device_id_type=MESH
-        )
-
-    barrier = pltpu.get_barrier_semaphore()
-    pl.semaphore_signal(barrier, inc=1, device_id=partner, device_id_type=MESH)
-
-    @pl.loop(1, n)
-    def _(t):
-        pl.semaphore_signal(barrier, inc=1, device_id=device(peer(t)), device_id_type=MESH)
-
-    pl.semaphore_wait(barrier, n)
-
+    scatter(1 - core)
     def owning(i, body):
         if everyone:
             body()
@@ -317,6 +341,7 @@
 
     swap = send(d_ref.at[1 - core], pair, psend, precv, partner)
     swap.start()
+    scatter(core)
     swap.wait()
 
     @pl.loop(0, held)
@@ -333,6 +358,8 @@
         if count > 0:
             part = ref.at[pl.ds(0, count)]
             pltpu.make_async_copy(part, part, sem).wait()
+
+    fetch.wait()
 
     def solve():
         wait_bytes(r, n - 1, srecv)
@@ -386,9 +413,17 @@
     forward = send(x_ref.at[core], x_ref.at[core], fsend, frecv, partner)
     forward.start()
     forward.wait()
-
-
-def post_kernel(G, M, bs, side, fe, s3, ae, x_ref, o_ref, lifted, sol):
+    fe_copy.wait()
+    s3_copy.wait()
+
+
+def post_kernel(G, M, bs, side, fe_hbm, s3_hbm, ae, x_ref, o_ref, lifted, sol, fe, s3, sems):
+    loads = [
+        pltpu.make_async_copy(s3_hbm, s3, sems.at[0]),
+        pltpu.make_async_copy(fe_hbm, fe, sems.at[1]),
+    ]
+    for c in loads:
+        c.start()
     Xe, Ye, K, Z = fe.shape
     X, Y = Xe - 2 * HALO, Ye - 2 * HALO
     bx, by, bz = X // CELL + 2, Y // CELL + 2, Z // CELL
@@ -408,7 +443,7 @@
         for i, group in rows:
             index = None
             for slot, j in enumerate(group):
-                packed = pick(ae[i, j], (lane % bz) * CELL)
+                packed = ae[i, j]
                 index = packed if index is None else jnp.where(lane // bz == slot, packed, index)
             inner.append(index % bs)
             outer.append(index // bs)
@@ -449,12 +484,14 @@
         lines(i * batch, batch)
 
     clear_outside(lifted, G, M, X, Y, HALO)
+    loads[0].wait()
 
     def start(x, y, c, near):
         sol[x, y] = s3[x, y] + ((1.0 - 6.0 * w) * c + w * near)
 
     sweep(lifted, 2, Xe - 2, 2, Ye - 2, start)
     clear_outside(sol, G, M, X, Y, 2)
+    loads[1].wait()
 
     def first(x, y, c, near):
         lifted[x, y] = (1.0 - 6.0 * w) * c + w * (fe[x, y] + near)
@@ -483,48 +520,40 @@
     owners = n_own * M
     sd = jax.ShapeDtypeStruct
 
-    wide_ids = jnp.broadcast_to(
-        jnp.repeat(aggregate, CELL, axis=2)[:, :, None, :], (bx, by, 8, Z)
-    )
-    fe, ae = pl.pallas_call(
-        functools.partial(halo_kernel, G, M),
-        out_shape=(sd((Xe, Ye, K, Z), F32), sd((bx + 2, by + 2, 8, Z), jnp.int32)),
-        in_specs=[vmem_spec()] * 2,
-        out_specs=(vmem_spec(),) * 2,
-        scratch_shapes=[pltpu.SemaphoreType.DMA((4,))] * 4
-        + [pltpu.SemaphoreType.DMA((4 * HALO,))] * 2,
+    fe, s3, ae, fix = pl.pallas_call(
+        functools.partial(down_kernel, G, M, n_own),
+        out_shape=(
+            sd((Xe, Ye, K, Z), F32),
+            sd((Xe, Ye, K, Z), F32),
+            sd((bx + 2, by + 2, 8, Z), jnp.int32),
+            sd((2, owners // 2, K, chunk), F32),
+        ),
+        in_specs=[vmem_spec(), vmem_spec(), any_spec()],
+        out_specs=(any_spec(), any_spec(), vmem_spec(), vmem_spec()),
+        scratch_shapes=[VMEM((Xe, Ye, K, Z), F32)] * 3
+        + [
+            VMEM((K, bx * by * bz), F32),
+            VMEM((2, owners // 2, chunk, bx * by * bz), BF16),
+            VMEM((2, owners // 2, K, chunk), F32),
+            VMEM((G * M // 2, K, chunk), F32),
+            VMEM((owners // 2, K, chunk), F32),
+            VMEM((owners // 2, K, chunk), F32),
+            VMEM((q, bs, bs), F32),
+        ]
+        + [pltpu.SemaphoreType.DMA((4,))] * 4
+        + [pltpu.SemaphoreType.DMA((4 * HALO,))] * 2
+        + [pltpu.SemaphoreType.DMA((3,))]
+        + [pltpu.SemaphoreType.DMA] * 8,
         compiler_params=params(collective_id=0, has_side_effects=True),
-        name="halo",
-    )(forcing, wide_ids)
-
-    s3, dense = pl.pallas_call(
-        functools.partial(pre_kernel, G, M, chunk, n_own // 2),
-        out_shape=(sd((Xe, Ye, K, Z), F32), sd((2, owners // 2, K, chunk), F32)),
-        in_specs=[vmem_spec()] * 2,
-        out_specs=(vmem_spec(),) * 2,
-        scratch_shapes=[VMEM((Xe, Ye, K, Z), F32), VMEM((K, bx * by * bz), F32)],
-        compiler_params=params(),
-        name="pre",
-    )(fe, aggregate.reshape(1, -1))
-
-    g = lax.axis_index("grp")
-    mine = lax.dynamic_slice_in_dim(factors, jnp.minimum(g, n_own - 1) * q, q, axis=0)
-    fix = pl.pallas_call(
-        functools.partial(coarse_kernel, G, M, n_own),
-        out_shape=sd((2, owners // 2, K, chunk), F32),
-        in_specs=[vmem_spec()] * 2,
-        out_specs=vmem_spec(),
-        scratch_shapes=[VMEM((G * M // 2, K, chunk), F32)] + [VMEM((owners // 2, K, chunk), F32)] * 2 + [pltpu.SemaphoreType.DMA] * 8,
-        compiler_params=params(collective_id=1, has_side_effects=True),
-        name="coarse",
-    )(dense, mine)
+        name="down",
+    )(forcing, aggregate, factors)
 
     return pl.pallas_call(
         functools.partial(post_kernel, G, M, bs, n_own // 2),
         out_shape=sd((K, X, Y, Z), F32),
-        in_specs=[vmem_spec()] * 4,
+        in_specs=[any_spec(), any_spec(), vmem_spec(), vmem_spec()],
         out_specs=vmem_spec(),
-        scratch_shapes=[VMEM((Xe, Ye, K, Z), F32)] * 2,
+        scratch_shapes=[VMEM((Xe, Ye, K, Z), F32)] * 4 + [pltpu.SemaphoreType.DMA((2,))],
         compiler_params=params(),
         name="post",
     )(fe, s3, ae, fix)

time: 90.8 us -> 74.6 us (0.82)
  Pallas kernels: 85.4 us -> 73.2 us
  local copies, waits for them, and re-layouts: 3.9 us -> 0 us
    pallas_call x3 -> x1, Pallas kernels: 64.3 us -> 55.1 us  [shards(): pl.pallas_call(functools.partial(down_kernel, G, M, n_own), out_shape=(sd...]
    pallas_call x1, Pallas kernels: 21 us -> 18.2 us  [shards(): pl.pallas_call(functools.partial(post_kernel, G, M, bs, n_own // 2), out_...]
    broadcast_in_dim x3 -> x0, local copies, waits for them, and re-layouts: 1.63 us -> none  [the longest x1 0.82 us: shards(): jnp.repeat(aggregate, CELL, axis=2)[:, :, None, :]]
    reshape x1 -> x0, local copies, waits for them, and re-layouts: 1.51 us -> none  [shards(): aggregate.reshape(1, -1)]
where the time goes in v3:
time: 74.6 us; the launch traced here: 73.2 us
  Pallas kernels  73.2 us (98%)
    pallas_call x1, Pallas kernels, shards(): pl.pallas_call(functools.partial(down_kernel, G, M, n_own), out_shape=(sd...  55.1 us
    pallas_call x1, Pallas kernels, shards(): pl.pallas_call(functools.partial(post_kernel, G, M, bs, n_own // 2), out_...  18.2 us

profile of v3, /device:TPU:8, one launch (start us, length us, event | category | flops | bytes accessed | tf_op | source)
XLA Modules:
  0.0 73.2 jit_solution(13242978219232396264)
XLA Ops:
  0.0 55.1 %down.1 = (f32[24,24,16,128]{3,2,1,0:T(8,128)}, f32[24,24,16,128]{3,2,1,0:T(8,128)}, s32[6,6,8,128]{3,2,1,0:T(8,128)}, f32[2,16,16,256]{3,2,1,0:T(8,128)}) custom-call(f32[16,16,16,128]{3,2,1,0:T(8,128)} %f_ref.1, s32[4,4,32]{2,1,0:T(4,128)} %a_ref.1, f32[32,128,128]{2,1,0:T(8,128)} %fac_hbm.1), custom_call_target="tpu_custom_call" | custom-call | tf_op jit(solution)/shard_map/down/pallas_call | solution.py:523
  55.1 18.2 %post.1 = f32[16,16,16,128]{3,2,1,0:T(8,128)} custom-call(f32[24,24,16,128]{3,2,1,0:T(8,128)} %get-tuple-element.9.fe_hbm, f32[24,24,16,128]{3,2,1,0:T(8,128)} %get-tuple-element.10.s3_hbm, s32[6,6,8,128]{3,2,1,0:T(8,128)} %get-tuple-element.11.ae, f32[2,16,16,256]{3,2,1,0:T(8,128)} %get-tuple-element.12.x_ref), custom_call_target="tpu_custom_call" | custom-call | tf_op jit(solution)/shard_map/post/pallas_call | solution.py:551

commit v4 on v3

--- a/solution.py
+++ b/solution.py
@@ -82,8 +82,8 @@
 
 
 def down_kernel(
-    G, M, n_own, f_ref, a_ref, fac_hbm, fe_out, s3_out, ae, x_ref,
-    fe, s3, s2, means, hot, d_ref, r, pair, e, fac_ref,
+    G, M, n_own, f_hbm, a_ref, fac_hbm, fe_out, s3_out, ae, x_ref,
+    f_ref, fe, s3, s2, res, means, hot, d_ref, r, pair, e, fac_ref,
     sx, rx, sy, ry, sc, rc, local, psend, precv, ssend, srecv, gsend, grecv, fsend, frecv,
 ):
     K, X, Y, Z = f_ref.shape
@@ -114,6 +114,8 @@
             src_ref=src, dst_ref=dst, send_sem=ssem, recv_sem=rsem, device_id=to, device_id_type=MESH
         )
 
+    load = pltpu.make_async_copy(f_hbm, f_ref, local.at[3])
+    load.start()
     barrier = pltpu.get_barrier_semaphore()
 
     def greet(to):
@@ -130,6 +132,7 @@
     first = lax.rem(g, n_own) * q
     fetch = pltpu.make_async_copy(fac_hbm.at[pl.ds(first, q)], fac_ref, local.at[0])
     fetch.start()
+    load.wait()
 
     @pl.loop(0, X)
     def _(x):
@@ -184,26 +187,36 @@
             device_id_type=MESH,
         )
 
+    near = HALO - 1
+
+    def across_axis(axis, d):
+        whole = pl.ds(HALO, (Y, X)[axis])
+        return (d, whole) if axis == 0 else (whole, d)
+
     def faces(down, axis, dev):
-        out = []
-        n, other = ((X, Y), (Y, X))[axis]
-        nb, otherb = ((bx, by), (by, bx))[axis]
-        for slot, (ref, h, length, across) in enumerate(
-            ((fe, HALO, n, other), (ae, 1, nb, otherb))
-        ):
-            src = pl.ds(h if down else length, h)
-            dst = pl.ds(length + h if down else 0, h)
-            whole = pl.ds(h, across)
-            pick = (lambda d: (d, whole)) if axis == 0 else (lambda d: (whole, d))
-            base = (0 if down else 2) + slot
-            out.append(copy(ref, pick(src), pick(dst), dev, (sx, rx) if axis == 0 else (sy, ry), base))
-        return out
+        n, nb, other = ((X, bx, by), (Y, by, bx))[axis]
+        sems = (sx, rx) if axis == 0 else (sy, ry)
+        base = 0 if down else 2
+        src = pl.ds(HALO if down else HALO + n - near, near)
+        dst = pl.ds(HALO + n if down else HALO - near, near)
+        out = [copy(fe, across_axis(axis, src), across_axis(axis, dst), dev, sems, base)]
+        src, dst = pl.ds(1 if down else nb, 1), pl.ds(1 + nb if down else 0, 1)
+        whole = pl.ds(1, other)
+        order = (lambda d: (d, whole)) if axis == 0 else (lambda d: (whole, d))
+        return out + [copy(ae, order(src), order(dst), dev, sems, base + 1)]
+
+    def far_faces(down, axis, dev):
+        n = (X, Y)[axis]
+        sems = (sx, rx) if axis == 0 else (sy, ry)
+        src = pl.ds(HALO + near if down else n, 1)
+        dst = pl.ds(HALO + n + near if down else 0, 1)
+        return [copy(fe, across_axis(axis, src), across_axis(axis, dst), dev, sems, 4 if down else 5)]
 
     def corners(down, dev):
         out = []
-        slot = 0 if down else 2 * HALO
-        for d in range(1, HALO):
-            width = HALO - d
+        slot = 0 if down else 4 * HALO
+        for d in range(1, near):
+            width = near - d
             src = pl.ds(HALO if down else HALO + Y - width, width)
             dst = pl.ds(HALO + Y if down else HALO - width, width)
             for row in (HALO - d, HALO + X - 1 + d):
@@ -216,39 +229,44 @@
             slot += 1
         return out
 
+    def far_corners(down, dev):
+        out = []
+        slot = (0 if down else 4 * HALO) + 2 * HALO
+        for d in range(1, HALO):
+            layer = HALO - d
+            src = pl.ds(HALO + layer - 1 if down else HALO + Y - layer, 1)
+            dst = pl.ds(HALO + Y + layer - 1 if down else HALO - layer, 1)
+            for row in (HALO - d, HALO + X - 1 + d):
+                out.append(copy(fe, (row, src), (row, dst), dev, (sc, rc), slot))
+                slot += 1
+        return out
+
     def each(index, count, name, body):
         if count > 1:
             pl.when(index > 0)(lambda: body(True, {name: index - 1}))
             pl.when(index < count - 1)(lambda: body(False, {name: index + 1}))
 
-    def start_faces(axis):
+    def begin(make):
         def body(down, dev):
-            for c in faces(down, axis, dev):
+            for c in make(down, dev):
                 c.start()
 
         return body
 
-    def end_faces(axis):
+    def end(make):
         def body(down, dev):
-            for c in faces(down, axis, dev):
+            for c in make(down, dev):
                 c.wait_send()
-            for c in faces(not down, axis, dev):
+            for c in make(not down, dev):
                 c.wait_recv()
 
         return body
 
-    def start_corners(down, dev):
-        for c in corners(down, dev):
-            c.start()
-
-    def end_corners(down, dev):
-        for c in corners(down, dev):
-            c.wait_send()
-        for c in corners(not down, dev):
-            c.wait_recv()
-
-    each(g, G, "grp", start_faces(0))
-    each(m, M, "mem", start_faces(1))
+    def along(make, axis):
+        return lambda down, dev: make(down, axis, dev)
+
+    each(g, G, "grp", begin(along(faces, 0)))
+    each(m, M, "mem", begin(along(faces, 1)))
 
 
     def second(x, y, c, near):
@@ -258,19 +276,34 @@
         s3[x, y] = (1.0 - 6.0 * w) * c + w * (fe[x, y] + near)
 
     def residual(x, y, c, near):
-        s2[x, y] = fe[x, y] - 6.0 * c + near
+        res[x - HALO, y - HALO] = fe[x, y] - 6.0 * c + near
 
     def inner(src, depth, emit):
         lo = HALO + depth
         sweep(src, lo, HALO + X - depth, lo, HALO + Y - depth, emit)
 
+    def halo_row(src, d, y0, y1, emit):
+        for x in (HALO - d, HALO + X - 1 + d):
+            sweep(src, x, x + 1, y0, y1, emit)
+
     def ring(src, depth, reach, emit):
         lo, hx, hy = HALO + depth, HALO + X - depth, HALO + Y - depth
         y0, y1 = HALO - reach, HALO + Y + reach
-        sweep(src, HALO - reach, lo, y0, y1, emit)
-        sweep(src, hx, HALO + X + reach, y0, y1, emit)
+        sweep(src, HALO, lo, y0, y1, emit)
+        sweep(src, hx, HALO + X, y0, y1, emit)
         sweep(src, lo, hx, y0, lo, emit)
         sweep(src, lo, hx, hy, y1, emit)
+        for d in range(1, reach + 1):
+            halo_row(src, d, y0 + d, y1 - d, emit)
+
+    def frame(src, reach, emit):
+        y0, y1 = HALO - reach, HALO + Y + reach
+        sweep(src, HALO, HALO + X, y0, y0 + 1, emit)
+        sweep(src, HALO, HALO + X, y1 - 1, y1, emit)
+        for d in range(1, reach):
+            halo_row(src, d, y0 + d, y0 + d + 1, emit)
+            halo_row(src, d, y1 - d - 1, y1 - d, emit)
+        halo_row(src, reach, HALO, HALO + Y, emit)
 
     inner(fe, 1, second)
     inner(s2, 2, third)
@@ -290,20 +323,18 @@
             hit = entry == ids - owner_of(c, h) * chunk
             hot[c, h] = jnp.where(hit, 1.0, 0.0).astype(BF16)
 
-    each(g, G, "grp", end_faces(0))
-    each(m, M, "mem", start_corners)
-    each(m, M, "mem", end_faces(1))
-    each(m, M, "mem", end_corners)
-
-    fe_copy = pltpu.make_async_copy(fe, fe_out, local.at[1])
-    fe_copy.start()
-
-    ring(fe, 1, 3, second)
-    clear_outside(s2, G, M, X, Y, 3)
-    ring(s2, 2, 2, third)
-    clear_outside(s3, G, M, X, Y, 2)
-    s3_copy = pltpu.make_async_copy(s3, s3_out, local.at[2])
-    s3_copy.start()
+    each(g, G, "grp", end(along(faces, 0)))
+    each(m, M, "mem", begin(corners))
+    each(m, M, "mem", end(along(faces, 1)))
+    each(g, G, "grp", begin(along(far_faces, 0)))
+    each(m, M, "mem", begin(along(far_faces, 1)))
+    each(m, M, "mem", end(corners))
+    each(m, M, "mem", begin(far_corners))
+
+    ring(fe, 1, 2, second)
+    clear_outside(s2, G, M, X, Y, 2)
+    ring(s2, 2, 1, third)
+    clear_outside(s3, G, M, X, Y, 1)
     inner(s3, 0, residual)
 
     rows = lax.broadcasted_iota(jnp.int32, (by * Z, by * bz), 0)
@@ -315,7 +346,7 @@
             total = None
             for p in range(CELL):
                 for t in range(CELL):
-                    v = s2[HALO + i * CELL + p, HALO + j * CELL + t]
+                    v = res[i * CELL + p, j * CELL + t]
                     total = v if total is None else total + v
             parts.append(total)
         line = jnp.concatenate(parts, axis=1)
@@ -359,6 +390,22 @@
             part = ref.at[pl.ds(0, count)]
             pltpu.make_async_copy(part, part, sem).wait()
 
+
+    each(g, G, "grp", end(along(far_faces, 0)))
+    each(m, M, "mem", end(along(far_faces, 1)))
+    each(m, M, "mem", end(far_corners))
+    fe_copy = pltpu.make_async_copy(
+        fe.at[pl.ds(HALO - 1, X + 2), pl.ds(HALO - 1, Y + 2)], fe_out, local.at[1]
+    )
+    fe_copy.start()
+    frame(fe, 3, second)
+    clear_outside(s2, G, M, X, Y, 3)
+    frame(s2, 2, third)
+    clear_outside(s3, G, M, X, Y, 2)
+    s3_copy = pltpu.make_async_copy(
+        s3.at[pl.ds(HALO - 2, X + 4), pl.ds(HALO - 2, Y + 4)], s3_out, local.at[2]
+    )
+    s3_copy.start()
     fetch.wait()
 
     def solve():
@@ -417,16 +464,16 @@
     s3_copy.wait()
 
 
-def post_kernel(G, M, bs, side, fe_hbm, s3_hbm, ae, x_ref, o_ref, lifted, sol, fe, s3, sems):
+def post_kernel(G, M, bs, side, fe_hbm, s3_hbm, ae, x_ref, o_hbm, lifted, sol, fe, s3, o_ref, sems):
+    Xe, Ye, K, Z = fe.shape
+    X, Y = Xe - 2 * HALO, Ye - 2 * HALO
+    bx, by, bz = X // CELL + 2, Y // CELL + 2, Z // CELL
     loads = [
-        pltpu.make_async_copy(s3_hbm, s3, sems.at[0]),
-        pltpu.make_async_copy(fe_hbm, fe, sems.at[1]),
+        pltpu.make_async_copy(s3_hbm, s3.at[pl.ds(HALO - 2, X + 4), pl.ds(HALO - 2, Y + 4)], sems.at[0]),
+        pltpu.make_async_copy(fe_hbm, fe.at[pl.ds(HALO - 1, X + 2), pl.ds(HALO - 1, Y + 2)], sems.at[1]),
     ]
     for c in loads:
         c.start()
-    Xe, Ye, K, Z = fe.shape
-    X, Y = Xe - 2 * HALO, Ye - 2 * HALO
-    bx, by, bz = X // CELL + 2, Y // CELL + 2, Z // CELL
     w = WEIGHT
     half = 8
     q = x_ref.shape[3] // bs
@@ -506,7 +553,15 @@
             1.0 - 6.0 * w
         ) * c + w * (fe[x, y] + near)
 
-    sweep(lifted, HALO, HALO + X, HALO, HALO + Y, last)
+    step = X // CELL
+    stores = []
+    for i in range(CELL):
+        sweep(lifted, HALO + i * step, HALO + (i + 1) * step, HALO, HALO + Y, last)
+        part = pl.ds(i * step, step)
+        stores.append(pltpu.make_async_copy(o_ref.at[:, part], o_hbm.at[:, part], sems.at[2 + i]))
+        stores[-1].start()
+    for c in stores:
+        c.wait()
 
 
 def shards(G, M, forcing, aggregate, factors):
@@ -523,15 +578,17 @@
     fe, s3, ae, fix = pl.pallas_call(
         functools.partial(down_kernel, G, M, n_own),
         out_shape=(
-            sd((Xe, Ye, K, Z), F32),
-            sd((Xe, Ye, K, Z), F32),
+            sd((X + 2, Y + 2, K, Z), F32),
+            sd((X + 4, Y + 4, K, Z), F32),
             sd((bx + 2, by + 2, 8, Z), jnp.int32),
             sd((2, owners // 2, K, chunk), F32),
         ),
-        in_specs=[vmem_spec(), vmem_spec(), any_spec()],
+        in_specs=[any_spec(), vmem_spec(), any_spec()],
         out_specs=(any_spec(), any_spec(), vmem_spec(), vmem_spec()),
-        scratch_shapes=[VMEM((Xe, Ye, K, Z), F32)] * 3
+        scratch_shapes=[VMEM((K, X, Y, Z), F32)]
+        + [VMEM((Xe, Ye, K, Z), F32)] * 3
         + [
+            VMEM((X, Y, K, Z), F32),
             VMEM((K, bx * by * bz), F32),
             VMEM((2, owners // 2, chunk, bx * by * bz), BF16),
             VMEM((2, owners // 2, K, chunk), F32),
@@ -540,9 +597,9 @@
             VMEM((owners // 2, K, chunk), F32),
             VMEM((q, bs, bs), F32),
         ]
-        + [pltpu.SemaphoreType.DMA((4,))] * 4
-        + [pltpu.SemaphoreType.DMA((4 * HALO,))] * 2
-        + [pltpu.SemaphoreType.DMA((3,))]
+        + [pltpu.SemaphoreType.DMA((6,))] * 4
+        + [pltpu.SemaphoreType.DMA((8 * HALO,))] * 2
+        + [pltpu.SemaphoreType.DMA((4,))]
         + [pltpu.SemaphoreType.DMA] * 8,
         compiler_params=params(collective_id=0, has_side_effects=True),
         name="down",
@@ -552,8 +609,9 @@
         functools.partial(post_kernel, G, M, bs, n_own // 2),
         out_shape=sd((K, X, Y, Z), F32),
         in_specs=[any_spec(), any_spec(), vmem_spec(), vmem_spec()],
-        out_specs=vmem_spec(),
-        scratch_shapes=[VMEM((Xe, Ye, K, Z), F32)] * 4 + [pltpu.SemaphoreType.DMA((2,))],
+        out_specs=any_spec(),
+        scratch_shapes=[VMEM((Xe, Ye, K, Z), F32)] * 4
+        + [VMEM((K, X, Y, Z), F32), pltpu.SemaphoreType.DMA((2 + CELL,))],
         compiler_params=params(),
         name="post",
     )(fe, s3, ae, fix)

time: 74.6 us -> 70.1 us (0.940)
  Pallas kernels: 73.2 us -> 69.2 us
    pallas_call x1, Pallas kernels: 55.1 us -> 51.5 us  [shards(): pl.pallas_call(functools.partial(down_kernel, G, M, n_own), out_shape=(sd...]
where the time goes in v4:
time: 70.1 us; the launch traced here: 69.2 us
  Pallas kernels  69.2 us (99%)
    pallas_call x1, Pallas kernels, shards(): pl.pallas_call(functools.partial(down_kernel, G, M, n_own), out_shape=(sd...  51.5 us
    pallas_call x1, Pallas kernels, shards(): pl.pallas_call(functools.partial(post_kernel, G, M, bs, n_own // 2), out_...  17.7 us

profile of v4, /device:TPU:8, one launch (start us, length us, event | category | flops | bytes accessed | tf_op | source)
XLA Modules:
  0.0 69.2 jit_solution(11338735235942649897)
XLA Ops:
  0.0 51.5 %down.1 = (f32[18,18,16,128]{3,2,1,0:T(8,128)}, f32[20,20,16,128]{3,2,1,0:T(8,128)}, s32[6,6,8,128]{3,2,1,0:T(8,128)}, f32[2,16,16,256]{3,2,1,0:T(8,128)}) custom-call(f32[16,16,16,128]{3,2,1,0:T(8,128)} %f_hbm.1, s32[4,4,32]{2,1,0:T(4,128)} %a_ref.1, f32[32,128,128]{2,1,0:T(8,128)} %fac_hbm.1), custom_call_target="tpu_custom_call" | custom-call | tf_op jit(solution)/shard_map/down/pallas_call | solution.py:578
  51.5 17.7 %post.1 = f32[16,16,16,128]{3,2,1,0:T(8,128)} custom-call(f32[18,18,16,128]{3,2,1,0:T(8,128)} %get-tuple-element.9.fe_hbm, f32[20,20,16,128]{3,2,1,0:T(8,128)} %get-tuple-element.10.s3_hbm, s32[6,6,8,128]{3,2,1,0:T(8,128)} %get-tuple-element.11.ae, f32[2,16,16,256]{3,2,1,0:T(8,128)} %get-tuple-element.12.x_ref), custom_call_target="tpu_custom_call" | custom-call | tf_op jit(solution)/shard_map/post/pallas_call | solution.py:608

commit v5 on v4

--- a/solution.py
+++ b/solution.py
@@ -134,10 +134,17 @@
     fetch.start()
     load.wait()
 
-    @pl.loop(0, X)
-    def _(x):
-        for y in range(Y):
-            fe[HALO + x, HALO + y] = flat[pl.ds(x * Y + y, K, stride=X * Y), :]
+    edge = HALO - 1
+
+    def turn(x0, x1, columns):
+        @pl.loop(x0, x1)
+        def _(x):
+            for y in columns:
+                fe[HALO + x, HALO + y] = flat[pl.ds(x * Y + y, K, stride=X * Y), :]
+
+    turn(0, edge, range(Y))
+    turn(X - edge, X, range(Y))
+    turn(edge, X - edge, [*range(edge), *range(Y - edge, Y)])
 
     for i in range(bx):
         for j in range(by):
@@ -267,6 +274,8 @@
 
     each(g, G, "grp", begin(along(faces, 0)))
     each(m, M, "mem", begin(along(faces, 1)))
+
+    turn(edge, X - edge, range(edge, Y - edge))
 
 
     def second(x, y, c, near):

time: 70.1 us -> 69.7 us (level)
  no operation moved by 1% of the time
where the time goes in v5:
time: 69.7 us; the launch traced here: 69 us
  Pallas kernels  69 us (99%)
    pallas_call x1, Pallas kernels, shards(): pl.pallas_call(functools.partial(down_kernel, G, M, n_own), out_shape=(sd...  51.3 us
    pallas_call x1, Pallas kernels, shards(): pl.pallas_call(functools.partial(post_kernel, G, M, bs, n_own // 2), out_...  17.7 us

profile of v5, /device:TPU:8, one launch (start us, length us, event | category | flops | bytes accessed | tf_op | source)
XLA Modules:
  0.0 69.0 jit_solution(12203559152575394796)
XLA Ops:
  0.0 51.3 %down.1 = (f32[18,18,16,128]{3,2,1,0:T(8,128)}, f32[20,20,16,128]{3,2,1,0:T(8,128)}, s32[6,6,8,128]{3,2,1,0:T(8,128)}, f32[2,16,16,256]{3,2,1,0:T(8,128)}) custom-call(f32[16,16,16,128]{3,2,1,0:T(8,128)} %f_hbm.1, s32[4,4,32]{2,1,0:T(4,128)} %a_ref.1, f32[32,128,128]{2,1,0:T(8,128)} %fac_hbm.1), custom_call_target="tpu_custom_call" | custom-call | tf_op jit(solution)/shard_map/down/pallas_call | solution.py:587
  51.3 17.7 %post.1 = f32[16,16,16,128]{3,2,1,0:T(8,128)} custom-call(f32[18,18,16,128]{3,2,1,0:T(8,128)} %get-tuple-element.9.fe_hbm, f32[20,20,16,128]{3,2,1,0:T(8,128)} %get-tuple-element.10.s3_hbm, s32[6,6,8,128]{3,2,1,0:T(8,128)} %get-tuple-element.11.ae, f32[2,16,16,256]{3,2,1,0:T(8,128)} %get-tuple-element.12.x_ref), custom_call_target="tpu_custom_call" | custom-call | tf_op jit(solution)/shard_map/post/pallas_call | solution.py:617
